TPU v7x, 32 devices: a whole 2x2x4 slice. The times are simulated.
32 devices in a mesh: seq: 16 (over z, x, core), batch: 2 (over y).
Axes of the slice: x: 2, y: 2, z: 4, core: 2. Of those that a mesh axis runs over, the one named last changes fastest.
Arguments:
- tokens: bfloat16 [2, 4096, 768], P('batch', 'seq'), may hold values from -6 to 6
- cotangent: bfloat16 [2, 4096, 768], P('batch', 'seq'), may hold values from -6 to 6
- bank: bfloat16 [2, 8192, 768], P('batch', 'seq'), may hold values from -6 to 6
- prefix: int32 [2], P('batch'), may hold values from 409 to 2048
- blocks: int32 [2, 8], P('batch'), may hold values from 0 to 63
- self_qkv: bfloat16 [768, 2304], P(('seq', 'batch')), may hold values from -0.21875 to 0.21875
- self_out: bfloat16 [768, 768], P(('seq', 'batch')), may hold values from -3.5 to 3.5
- cross_q: bfloat16 [768, 768], P(('seq', 'batch')), may hold values from -0.21875 to 0.21875
- cross_kv: bfloat16 [768, 1536], P(('seq', 'batch')), may hold values from -0.21875 to 0.21875
- cross_out: bfloat16 [768, 768], P(('seq', 'batch')), may hold values from -1.75 to 1.75
- ffn_in: bfloat16 [768, 3072], P(('seq', 'batch')), may hold values from -0.21875 to 0.21875
- ffn_out: bfloat16 [3072, 768], P(('seq', 'batch')), may hold values from -0.109375 to 0.109375
- gains: bfloat16 [3, 768], P(None, ('seq', 'batch')), may hold values from 0.5 to 1.5
- biases: bfloat16 [14, 768], P(None, ('seq', 'batch')), may hold values from -1.75 to 1.75
Outputs:
- output: bfloat16 [2, 4096, 768], P('batch', 'seq')
- tokens_grad: float32 [2, 4096, 768], P('batch', 'seq')
- bank_grad: float32 [2, 8192, 768], P('batch', 'seq')
- self_qkv_grad: float32 [768, 2304], P(('seq', 'batch'))
- self_out_grad: float32 [768, 768], P(('seq', 'batch'))
- cross_q_grad: float32 [768, 768], P(('seq', 'batch'))
- cross_kv_grad: float32 [768, 1536], P(('seq', 'batch'))
- cross_out_grad: float32 [768, 768], P(('seq', 'batch'))
- ffn_in_grad: float32 [768, 3072], P(('seq', 'batch'))
- ffn_out_grad: float32 [3072, 768], P(('seq', 'batch'))
- gains_grad: float32 [3, 768], P(None, ('seq', 'batch'))
- biases_grad: float32 [14, 768], P(None, ('seq', 'batch'))
All inputs are finite; a program needn't handle non-finite values.
Results may differ from a plain program's by a relative error of at most 0.025.
Values may be sent and summed in bfloat16 or wider, within the bound.
No kernel may reach another device: no remote copies, remote signals or barrier semaphores. Data moves between devices by JAX's collectives and lax.ppermute only.
A program may use at most 256 MiB of HBM per device.

v0:
```python
import jax
import jax.numpy as jnp
from jax import lax
from jax.sharding import PartitionSpec as P

HEADS = 12
HEAD_DIM = 64
BANK_DEV = 512
BANK_BLOCK = 128


EPSILON = 1e-05
NEGATIVE = -1e30
PRECISE = lax.Precision.HIGHEST


def layer_norm(values, gain, shift):
    centered = values - jnp.mean(values, axis=-1, keepdims=True)
    variance = jnp.mean(centered * centered, axis=-1, keepdims=True)
    return centered * lax.rsqrt(variance + EPSILON) * gain + shift


def gelu_exact(values):
    return jax.nn.gelu(values, approximate=False)


def rounded(values):
    return values.astype(jnp.bfloat16)


def matmul(left, right):
    return jnp.dot(left, right, preferred_element_type=jnp.float32)


def weight_grad(left, right):
    return lax.dot_general(
        left, right, (((0,), (0,)), ((), ())), preferred_element_type=jnp.float32
    )


def back_matmul(left, right):
    return lax.dot_general(
        left, right, (((1,), (1,)), ((), ())), preferred_element_type=jnp.float32
    )


def split_heads(matrix):
    return matrix.reshape(matrix.shape[0], HEADS, HEAD_DIM)


def column_sums(values):
    return jnp.sum(values.astype(jnp.float32), axis=0)


def masked_scores(query_heads, key_rows, query_pos, key_pos, prefix_len):
    scores = jnp.einsum(
        "qhd,khd->hqk", query_heads, split_heads(key_rows), preferred_element_type=jnp.float32
    ) * HEAD_DIM ** (-0.5)
    allowed = (key_pos[None, :] <= query_pos[:, None]) | (key_pos[None, :] < prefix_len)
    return jnp.where(allowed[None], scores, NEGATIVE)


def key_block_count(first_row, rows, prefix_len, key_block):
    needed = jnp.maximum(first_row + rows, prefix_len)
    return (needed + key_block - 1) // key_block


def self_forward(query, keyval_all, first_row, prefix_len):
    rows, width = query.shape
    length = keyval_all.shape[0]
    key_block = min(512, length)
    query_heads = split_heads(query)
    query_pos = first_row + jnp.arange(rows, dtype=jnp.int32)
    block_count = key_block_count(first_row, rows, prefix_len, key_block)

    def block_scores(block_index):
        key_first = block_index * key_block
        block_rows = lax.dynamic_slice_in_dim(keyval_all, key_first, key_block, 0)
        key_pos = key_first + jnp.arange(key_block, dtype=jnp.int32)
        return (
            masked_scores(query_heads, block_rows[:, :width], query_pos, key_pos, prefix_len),
            block_rows,
        )

    def totals_step(block_index, carry):
        running_max, running_sum = carry
        scores, block_rows = block_scores(block_index)
        new_max = jnp.maximum(running_max, jnp.max(scores, axis=-1))
        new_sum = running_sum * jnp.exp(running_max - new_max) + jnp.sum(
            jnp.exp(scores - new_max[..., None]), axis=-1
        )
        return (new_max, new_sum)

    start_max = jnp.full((HEADS, rows), NEGATIVE, jnp.float32)
    start_sum = jnp.zeros((HEADS, rows), jnp.float32)
    running_max, running_sum = lax.fori_loop(0, block_count, totals_step, (start_max, start_sum))
    log_total = running_max + jnp.log(running_sum)

    def output_step(block_index, accum):
        scores, block_rows = block_scores(block_index)
        probs_low = rounded(jnp.exp(scores - log_total[..., None]))
        return accum + jnp.einsum(
            "hqk,khd->qhd",
            probs_low,
            split_heads(block_rows[:, width:]),
            preferred_element_type=jnp.float32,
        )

    accum = lax.fori_loop(
        0, block_count, output_step, jnp.zeros((rows, HEADS, HEAD_DIM), jnp.float32)
    )
    return (accum.reshape(rows, width), log_total)


def query_backward(query, keyval_all, datt_low, log_total, delta, first_row, prefix_len):
    rows, width = query.shape
    length = keyval_all.shape[0]
    key_block = min(512, length)
    scale = HEAD_DIM ** (-0.5)
    query_heads = split_heads(query)
    grad_heads = split_heads(datt_low)
    query_pos = first_row + jnp.arange(rows, dtype=jnp.int32)
    block_count = key_block_count(first_row, rows, prefix_len, key_block)

    def grad_step(block_index, carry):
        query_grad, key_grads = carry
        key_first = block_index * key_block
        block_rows = lax.dynamic_slice_in_dim(keyval_all, key_first, key_block, 0)
        key_pos = key_first + jnp.arange(key_block, dtype=jnp.int32)
        scores = masked_scores(query_heads, block_rows[:, :width], query_pos, key_pos, prefix_len)
        probs = jnp.exp(scores - log_total[..., None])
        key_heads = split_heads(block_rows[:, :width])
        value_heads = split_heads(block_rows[:, width:])
        prob_grad = jnp.einsum(
            "qhd,khd->hqk", grad_heads, value_heads, preferred_element_type=jnp.float32
        )
        score_low = rounded(probs * (prob_grad - delta[..., None]))
        query_grad = (
            query_grad
            + jnp.einsum("hqk,khd->qhd", score_low, key_heads, preferred_element_type=jnp.float32)
            * scale
        )
        key_part = (
            jnp.einsum("hqk,qhd->khd", score_low, query_heads, preferred_element_type=jnp.float32)
            * scale
        )
        value_part = jnp.einsum(
            "hqk,qhd->khd", rounded(probs), grad_heads, preferred_element_type=jnp.float32
        )
        update = jnp.concatenate(
            [key_part.reshape(key_block, width), value_part.reshape(key_block, width)], axis=1
        )
        key_grads = lax.dynamic_update_slice_in_dim(key_grads, update, key_first, 0)
        return (query_grad, key_grads)

    start_keys = jnp.zeros((length, 2 * width), jnp.float32)
    start = (jnp.zeros((rows, HEADS, HEAD_DIM), jnp.float32), start_keys)
    query_grad, key_grads = lax.fori_loop(0, block_count, grad_step, start)
    return (query_grad.reshape(rows, width), key_grads)


def body(
    tokens,
    cotangent,
    bank,
    prefix,
    blocks,
    self_qkv,
    self_out,
    cross_q,
    cross_kv,
    cross_out,
    ffn_in,
    ffn_out,
    gains,
    biases,
):
    forward_full = (
        lax.all_gather(self_qkv, ("seq", "batch"), axis=0, tiled=True),
        lax.all_gather(self_out, ("seq", "batch"), axis=0, tiled=True),
        lax.all_gather(cross_q, ("seq", "batch"), axis=0, tiled=True),
        lax.all_gather(cross_kv, ("seq", "batch"), axis=0, tiled=True),
        lax.all_gather(cross_out, ("seq", "batch"), axis=0, tiled=True),
        lax.all_gather(ffn_in, ("seq", "batch"), axis=0, tiled=True),
        lax.all_gather(ffn_out, ("seq", "batch"), axis=0, tiled=True),
        lax.all_gather(gains, ("seq", "batch"), axis=1, tiled=True),
        lax.all_gather(biases, ("seq", "batch"), axis=1, tiled=True),
    )
    (
        qkv_full,
        selfout_full,
        crossq_full,
        crosskv_full,
        crossout_full,
        ffnin_full,
        ffnout_full,
        gain_full,
        bias_full,
    ) = forward_full
    seq_index = lax.axis_index("seq")
    rows = tokens.shape[1]
    width = tokens.shape[2]
    scale = HEAD_DIM ** (-0.5)
    first_row = seq_index * rows
    prefix_len = prefix[0]
    inputs = tokens[0]
    inputs_wide = inputs.astype(jnp.float32)
    gain_wide = gain_full.astype(jnp.float32)
    bias_wide = bias_full.astype(jnp.float32)
    zero_row = jnp.zeros((width,), jnp.float32)
    qkv = rounded(
        matmul(inputs, qkv_full) + jnp.concatenate([bias_wide[3], zero_row, bias_wide[4]])
    )
    query = qkv[:, :width]
    keyval = qkv[:, width:]
    keyval_all = lax.all_gather(keyval, "seq", axis=0, tiled=True)
    attention, log_total = self_forward(query, keyval_all, first_row, prefix_len)
    attention_low = rounded(attention)
    resid_one = inputs_wide + matmul(attention_low, selfout_full) + bias_wide[5]
    hidden_one = layer_norm(resid_one, gain_wide[0], bias_wide[0])
    hidden_one_low = rounded(hidden_one)
    cross_query = rounded(matmul(hidden_one_low, crossq_full) + bias_wide[6])
    local_blocks = BANK_DEV // BANK_BLOCK
    bank_blocks = bank[0].reshape(local_blocks, BANK_BLOCK, width)
    local_ids = blocks[0] - seq_index * local_blocks
    selector = local_ids[:, None] == jnp.arange(local_blocks, dtype=jnp.int32)[None, :]
    picked = jnp.einsum(
        "hn,nos->hos",
        selector.astype(jnp.bfloat16),
        bank_blocks,
        preferred_element_type=jnp.float32,
    ).reshape(-1, width)
    own_rows = rounded(
        lax.psum_scatter(
            picked.astype(jnp.bfloat16), "seq", scatter_dimension=0, tiled=True
        ).astype(jnp.float32)
    )
    cross_part = rounded(matmul(own_rows, crosskv_full) + jnp.concatenate([zero_row, bias_wide[7]]))
    cross_all = lax.all_gather(cross_part, "seq", axis=0, tiled=True)
    cquery_heads = split_heads(cross_query)
    ckey_heads = split_heads(cross_all[:, :width])
    cvalue_heads = split_heads(cross_all[:, width:])
    cross_scores = (
        jnp.einsum("qhd,khd->hqk", cquery_heads, ckey_heads, preferred_element_type=jnp.float32)
        * scale
    )
    cross_exp = jnp.exp(cross_scores - jnp.max(cross_scores, axis=-1, keepdims=True))
    cross_probs = cross_exp / jnp.sum(cross_exp, axis=-1, keepdims=True)
    cross_probs_low = rounded(cross_probs)
    cross_att = rounded(
        jnp.einsum(
            "hqk,khd->qhd", cross_probs_low, cvalue_heads, preferred_element_type=jnp.float32
        ).reshape(rows, width)
    )
    resid_two = hidden_one + matmul(cross_att, crossout_full) + bias_wide[8]
    hidden_two = layer_norm(resid_two, gain_wide[1], bias_wide[1])
    hidden_two_low = rounded(hidden_two)
    inner = matmul(hidden_two_low, ffnin_full) + bias_wide[10:14].reshape(-1)
    activated = rounded(gelu_exact(inner))
    resid_three = hidden_two + matmul(activated, ffnout_full) + bias_wide[9]
    output = layer_norm(resid_three, gain_wide[2], bias_wide[2])
    backward_full = (
        lax.all_gather(self_qkv, ("seq", "batch"), axis=0, tiled=True),
        lax.all_gather(self_out, ("seq", "batch"), axis=0, tiled=True),
        lax.all_gather(cross_q, ("seq", "batch"), axis=0, tiled=True),
        lax.all_gather(cross_kv, ("seq", "batch"), axis=0, tiled=True),
        lax.all_gather(cross_out, ("seq", "batch"), axis=0, tiled=True),
        lax.all_gather(ffn_in, ("seq", "batch"), axis=0, tiled=True),
        lax.all_gather(ffn_out, ("seq", "batch"), axis=0, tiled=True),
        lax.all_gather(gains, ("seq", "batch"), axis=1, tiled=True),
        lax.all_gather(biases, ("seq", "batch"), axis=1, tiled=True),
    )
    (
        qkv_back,
        selfout_back,
        crossq_back,
        crosskv_back,
        crossout_back,
        ffnin_back,
        ffnout_back,
        gain_back,
        bias_back,
    ) = backward_full
    gain_again = gain_back.astype(jnp.float32)
    bias_again = bias_back.astype(jnp.float32)
    _unused, norm_three = jax.vjp(layer_norm, resid_three, gain_again[2], bias_again[2])
    dresid_three, dgain_three, dshift_three = norm_three(cotangent[0].astype(jnp.float32))
    douter_low = rounded(dresid_three)
    grad_ffnout = weight_grad(activated, douter_low)
    _unused, gelu_back = jax.vjp(gelu_exact, inner)
    dinner_low = rounded(gelu_back(back_matmul(douter_low, ffnout_back))[0])
    grad_ffnin = weight_grad(hidden_two_low, dinner_low)
    _unused, norm_two = jax.vjp(layer_norm, resid_two, gain_again[1], bias_again[1])
    dresid_two, dgain_two, dshift_two = norm_two(dresid_three + back_matmul(dinner_low, ffnin_back))
    dcross_low = rounded(dresid_two)
    grad_crossout = weight_grad(cross_att, dcross_low)
    dcross_att = rounded(back_matmul(dcross_low, crossout_back))
    dcross_heads = split_heads(dcross_att)
    dcross_probs = jnp.einsum(
        "qhd,khd->hqk", dcross_heads, cvalue_heads, preferred_element_type=jnp.float32
    )
    dcross_scores = rounded(
        cross_probs * (dcross_probs - jnp.sum(cross_probs * dcross_probs, axis=-1, keepdims=True))
    )
    dcross_query = rounded(
        jnp.einsum(
            "hqk,khd->qhd", dcross_scores, ckey_heads, preferred_element_type=jnp.float32
        ).reshape(rows, width)
        * scale
    )
    dcross_key = (
        jnp.einsum("hqk,qhd->khd", dcross_scores, cquery_heads, preferred_element_type=jnp.float32)
        * scale
    )
    dcross_value = jnp.einsum(
        "hqk,qhd->khd", cross_probs_low, dcross_heads, preferred_element_type=jnp.float32
    )
    dcross_all = jnp.concatenate(
        [dcross_key.reshape(-1, width), dcross_value.reshape(-1, width)], axis=1
    )
    dcross_pair = rounded(
        lax.psum_scatter(
            dcross_all.astype(jnp.bfloat16), "seq", scatter_dimension=0, tiled=True
        ).astype(jnp.float32)
    )
    grad_crossq = weight_grad(hidden_one_low, dcross_query)
    grad_crosskv = weight_grad(own_rows, dcross_pair)
    drows_own = back_matmul(dcross_pair, crosskv_back)
    drows = lax.all_gather(drows_own.astype(jnp.bfloat16), "seq", axis=0, tiled=True).astype(
        drows_own.dtype
    )
    bank_grad = jnp.einsum(
        "lx,lut->xut",
        selector.astype(jnp.float32),
        drows.reshape(-1, BANK_BLOCK, width),
        precision=PRECISE,
    ).reshape(-1, width)
    _unused, norm_one = jax.vjp(layer_norm, resid_one, gain_again[0], bias_again[0])
    dresid_one, dgain_one, dshift_one = norm_one(
        dresid_two + back_matmul(dcross_query, crossq_back)
    )
    dbranch_low = rounded(dresid_one)
    grad_selfout = weight_grad(attention_low, dbranch_low)
    datt_low = rounded(back_matmul(dbranch_low, selfout_back))
    delta = jnp.sum(
        (datt_low.astype(jnp.float32) * attention).reshape(rows, HEADS, HEAD_DIM), axis=-1
    ).T
    keys_again = lax.all_gather(keyval, "seq", axis=0, tiled=True)
    dquery, dkey_all = query_backward(
        query, keys_again, datt_low, log_total, delta, first_row, prefix_len
    )
    dkeyval = lax.psum_scatter(
        dkey_all.astype(jnp.bfloat16), "seq", scatter_dimension=0, tiled=True
    ).astype(jnp.float32)
    dqkv = rounded(jnp.concatenate([dquery, dkeyval], axis=1))
    grad_qkv = weight_grad(inputs, dqkv)
    tokens_grad = dresid_one + back_matmul(dqkv, qkv_back)
    dqkv_sums = column_sums(dqkv)
    dpair_sums = column_sums(dcross_pair)
    gain_grad = jnp.stack([dgain_one, dgain_two, dgain_three])
    bias_head = jnp.stack(
        [
            dshift_one,
            dshift_two,
            dshift_three,
            dqkv_sums[:width],
            dqkv_sums[2 * width :],
            column_sums(dbranch_low),
            column_sums(dcross_query),
            dpair_sums[width:],
            column_sums(dcross_low),
            column_sums(douter_low),
        ]
    )
    bias_grad = jnp.concatenate([bias_head, column_sums(dinner_low).reshape(-1, width)], axis=0)
    reduced = (
        lax.psum_scatter(grad_qkv, ("seq", "batch"), scatter_dimension=0, tiled=True),
        lax.psum_scatter(grad_selfout, ("seq", "batch"), scatter_dimension=0, tiled=True),
        lax.psum_scatter(grad_crossq, ("seq", "batch"), scatter_dimension=0, tiled=True),
        lax.psum_scatter(grad_crosskv, ("seq", "batch"), scatter_dimension=0, tiled=True),
        lax.psum_scatter(grad_crossout, ("seq", "batch"), scatter_dimension=0, tiled=True),
        lax.psum_scatter(grad_ffnin, ("seq", "batch"), scatter_dimension=0, tiled=True),
        lax.psum_scatter(grad_ffnout, ("seq", "batch"), scatter_dimension=0, tiled=True),
        lax.psum_scatter(gain_grad, ("seq", "batch"), scatter_dimension=1, tiled=True),
        lax.psum_scatter(bias_grad, ("seq", "batch"), scatter_dimension=1, tiled=True),
    )
    return (
        rounded(output)[None],
        tokens_grad[None],
        bank_grad[None],
        reduced[0],
        reduced[1],
        reduced[2],
        reduced[3],
        reduced[4],
        reduced[5],
        reduced[6],
        reduced[7],
        reduced[8],
    )


def solution(mesh):
    return jax.shard_map(
        body,
        mesh=mesh,
        in_specs=(
            P("batch", "seq", None),
            P("batch", "seq", None),
            P("batch", "seq", None),
            P("batch"),
            P("batch", None),
            P(("seq", "batch"), None),
            P(("seq", "batch"), None),
            P(("seq", "batch"), None),
            P(("seq", "batch"), None),
            P(("seq", "batch"), None),
            P(("seq", "batch"), None),
            P(("seq", "batch"), None),
            P(None, ("seq", "batch")),
            P(None, ("seq", "batch")),
        ),
        out_specs=(
            P("batch", "seq", None),
            P("batch", "seq", None),
            P("batch", "seq", None),
            P(("seq", "batch"), None),
            P(("seq", "batch"), None),
            P(("seq", "batch"), None),
            P(("seq", "batch"), None),
            P(("seq", "batch"), None),
            P(("seq", "batch"), None),
            P(("seq", "batch"), None),
            P(None, ("seq", "batch")),
            P(None, ("seq", "batch")),
        ),
        check_vma=False,
    )
```

profile of v0, /device:TPU:0, one launch (start us, length us, event | category | flops | bytes accessed | tf_op | source)
XLA Modules:
  0.0 1761.0 jit_solution(6879612047977391814)
XLA Ops:
  12.7 71.1 %all-gather = bf16[32,24,14]{1,2,0:T(8,128)(2,1)S(1)} all-gather(bf16[1,24,14]{1,2,0:T(8,128)(2,1)S(1)} %bitcast.291), channel_id=1, replica_groups=mesh['seq'=16,'batch'=2] {'seq','batch'}, dimensions={0}, use_global_device_ids=true | all-gather | bytes 22176 | tf_op jit(solution)/shard_map/all_gather | solution.py:187
  84.2 63.6 %all-gather.1 = bf16[32,24,3]{1,2,0:T(4,128)(2,1)S(1)} all-gather(bf16[1,24,3]{1,2,0:T(4,128)(2,1)S(1)} %bitcast.292), channel_id=1, replica_groups=mesh['seq'=16,'batch'=2] {'seq','batch'}, dimensions={0}, use_global_device_ids=true | all-gather | bytes 4752 | tf_op jit(solution)/shard_map/all_gather | solution.py:186
  160.8 34.5 %all-gather.21.cloned.1.call-done = bf16[1024,1536]{1,0:T(8,128)(2,1)} async-done(((bf16[64,1536]{1,0:T(8,128)(2,1)}), bf16[1024,1536]{1,0:T(8,128)(2,1)}) %all-gather.21.cloned.1.call-update) | async-done | bytes 3145744 | tf_op jit(solution)/shard_map/all_gather | solution.py:239
  202.7 94.1 %all-gather.15.cloned.1.call-done = bf16[4096,1536]{1,0:T(8,128)(2,1)} async-done(((bf16[256,1536]{1,0:T(8,128)(2,1)}), bf16[4096,1536]{1,0:T(8,128)(2,1)}) %all-gather.15.cloned.1.call-update) | async-done | bytes 12582928 | tf_op jit(solution)/shard_map/all_gather | solution.py:216
  296.9 16.8 copy.99
  313.7 13.8 while.37
  327.6 13.9 while.38
  354.3 53.8 %all-gather.23.cloned.1.call-done = bf16[768,768]{1,0:T(8,128)(2,1)} async-done(((bf16[24,768]{1,0:T(8,128)(2,1)}), bf16[768,768]{1,0:T(8,128)(2,1)}) %all-gather.23.cloned.1.call-update) | async-done | bytes 1179664 | tf_op jit(solution)/shard_map/all_gather | solution.py:181
  426.8 37.1 %all-gather.25.cloned.1.call-done = bf16[768,768]{1,0:T(8,128)(2,1)} async-done(((bf16[24,768]{1,0:T(8,128)(2,1)}), bf16[768,768]{1,0:T(8,128)(2,1)}) %all-gather.25.cloned.1.call-update) | async-done | bytes 1179664 | tf_op jit(solution)/shard_map/all_gather | solution.py:183
  466.0 63.0 %all-gather.27.cloned.1.call-done = bf16[768,3072]{1,0:T(8,128)(2,1)} async-done(((bf16[24,3072]{1,0:T(8,128)(2,1)}), bf16[768,3072]{1,0:T(8,128)(2,1)}) %all-gather.27.cloned.1.call-update) | async-done | bytes 4718608 | tf_op jit(solution)/shard_map/all_gather | solution.py:184
  529.0 12.0 multiply_convert_fusion.2
  541.0 52.6 %all-gather.29.cloned.1.call-done = bf16[3072,768]{1,0:T(8,128)(2,1)} async-done(((bf16[96,768]{1,0:T(8,128)(2,1)}), bf16[3072,768]{1,0:T(8,128)(2,1)}) %all-gather.29.cloned.1.call-update) | async-done | bytes 4718608 | tf_op jit(solution)/shard_map/all_gather | solution.py:185
  662.3 31.2 %while.39 = (s32[]{:T(128)}, f32[256,12,64]{0,2,1:T(8,128)S(1)}, bf16[4096,1536]{0,1:T(8,128)(2,1)}, s32[]{:T(128)}, bf16[4096,1536]{0,1:T(8,128)(2,1)}, /*index...) while((s32[]{:T(128)}, f32[256,12,64]{0,2,1:T(8,128)S(1)}, ...), condition=%wide.region_24.25_spmd.clone, body=%wide.region_23.24_spmd.clone.sunk | while | flops 1026950912 | bytes 42118388 | solution.py:158
  693.6 25.9 %reduce-scatter.33.cloned.1.call-done = bf16[64,1536]{1,0:T(8,128)(2,1)} async-done(((bf16[1024,1536]{1,0:T(8,128)(2,1)}), bf16[64,1536]{1,0:T(8,128)(2,1)}) %reduce-scatter.33.cloned.1.call-update) | async-done | bytes 196624
  747.3 130.9 %reduce-scatter.19.cloned.1.call-done = bf16[256,1536]{0,1:T(8,128)(2,1)} async-done(((bf16[4096,1536]{0,1:T(8,128)(2,1)}), bf16[256,1536]{0,1:T(8,128)(2,1)}) %reduce-scatter.19.cloned.1.call-update) | async-done | bytes 786448 | tf_op jit(solution)/shard_map/reduce_scatter | solution.py:352
  893.2 26.6 %all-gather.31.cloned.1.call-done = bf16[1024,768]{1,0:T(8,128)(2,1)} async-done(((bf16[64,768]{1,0:T(8,128)(2,1)}), bf16[1024,768]{1,0:T(8,128)(2,1)}) %all-gather.31.cloned.1.call-update) | async-done | bytes 1572880 | tf_op jit(solution)/shard_map/all_gather | solution.py:329
  924.4 39.0 %all-reduce.3 = (f32[3,768]{1,0:T(4,128)S(1)}, f32[14,768]{1,0:T(8,128)S(1)}) all-reduce(f32[3,768]{1,0:T(4,128)S(1)} %pad_maximum_fusion.5, f32[14,768]{1,0:T(8,128)S(1)} %concatenate.24), channel_id=12, replica_groups=mesh['seq'=16,'batch'=2] {'seq','batch'}, use_global_device_ids=true, to_apply=%region_37.38.clone | all-reduce | flops 13056 | bytes 104448
  968.7 55.1 %reduce-scatter.21.cloned.1.call-done = f32[24,768]{1,0:T(8,128)} async-done(((f32[768,768]{1,0:T(8,128)}), f32[24,768]{1,0:T(8,128)}) %reduce-scatter.21.cloned.1.call-update) | async-done | bytes 73744 | tf_op jit(solution)/shard_map/reduce_scatter | solution.py:378
  1023.9 104.4 %reduce-scatter.23.cloned.1.call-done = f32[24,768]{1,0:T(8,128)} async-done(((f32[768,768]{1,0:T(8,128)}), f32[24,768]{1,0:T(8,128)}) %reduce-scatter.23.cloned.1.call-update) | async-done | bytes 73744 | tf_op jit(solution)/shard_map/reduce_scatter | solution.py:379
  1128.2 104.5 %reduce-scatter.27.cloned.1.call-done = f32[24,768]{1,0:T(8,128)} async-done(((f32[768,768]{1,0:T(8,128)}), f32[24,768]{1,0:T(8,128)}) %reduce-scatter.27.cloned.1.call-update) | async-done | bytes 73744 | tf_op jit(solution)/shard_map/reduce_scatter | solution.py:381
  1232.7 112.6 %reduce-scatter.25.cloned.1.call-done = f32[24,1536]{1,0:T(8,128)} async-done(((f32[768,1536]{1,0:T(8,128)}), f32[24,1536]{1,0:T(8,128)}) %reduce-scatter.25.cloned.1.call-update) | async-done | bytes 147472 | tf_op jit(solution)/shard_map/reduce_scatter | solution.py:380
  1345.4 141.7 %reduce-scatter.29.cloned.1.call-done = f32[24,3072]{1,0:T(8,128)} async-done(((f32[768,3072]{1,0:T(8,128)}), f32[24,3072]{1,0:T(8,128)}) %reduce-scatter.29.cloned.1.call-update) | async-done | bytes 294928 | tf_op jit(solution)/shard_map/reduce_scatter | solution.py:382
  1487.1 141.5 %reduce-scatter.31.cloned.1.call-done = f32[96,768]{1,0:T(8,128)} async-done(((f32[3072,768]{1,0:T(8,128)}), f32[96,768]{1,0:T(8,128)}) %reduce-scatter.31.cloned.1.call-update) | async-done | bytes 294928 | tf_op jit(solution)/shard_map/reduce_scatter | solution.py:383
  1628.6 124.8 %reduce-scatter.35.cloned.1.call-done = f32[24,2304]{1,0:T(8,128)} async-done(((f32[768,2304]{1,0:T(8,128)}), f32[24,2304]{1,0:T(8,128)}) %reduce-scatter.35.cloned.1.call-update) | async-done | bytes 221200
  (418 shorter events, 236.5 us)
Async XLA Ops:
  8.0 140.8 %reduce-scatter.17.cloned.1.call-start = ((), (), s32[]{:S(2)}) async-start(), calls=%async_computation.13 | async-start | bytes 1671168 | tf_op jit(solution)/shard_map/reduce_scatter | solution.py:234
  11.4 140.5 %copy-start.26 = (bf16[1,256,768]{2,1,0:T(8,128)(2,1)S(1)}, bf16[1,256,768]{2,1,0:T(8,128)(2,1)}, u32[]{:S(2)}) copy-start(bf16[1,256,768]{2,1,0:T(8,128)(2,1)} %param.20) | copy-start | bytes 1179652
  11.4 137.4 %all-gather.19.cloned.1.call-start = ((), (), s32[]{:S(2)}) async-start(), calls=%async_computation.14 | async-start | bytes 2433024 | tf_op jit(solution)/shard_map/all_gather | solution.py:182
  12.0 139.9 %all-gather.13.cloned.1.call-start = ((), (), s32[]{:S(2)}) async-start(), calls=%async_computation.10 | async-start | bytes 3649536 | tf_op jit(solution)/shard_map/all_gather | solution.py:179
  12.6 182.7 %all-gather.21.cloned.1.call-start = ((), (), s32[]{:S(2)}) async-start(), calls=%async_computation.15 | async-start | bytes 3342336 | tf_op jit(solution)/shard_map/all_gather | solution.py:239
  151.8 145.1 %all-gather.15.cloned.1.call-start = ((), (), s32[]{:S(2)}) async-start(), calls=%async_computation.11 | async-start | bytes 13369344 | tf_op jit(solution)/shard_map/all_gather | solution.py:216
  156.0 196.1 %all-gather.17.cloned.1.call-start = ((), (), s32[]{:S(2)}) async-start(), calls=%async_computation.12 | async-start | bytes 1216512 | tf_op jit(solution)/shard_map/all_gather | solution.py:180
  156.8 251.3 %all-gather.23.cloned.1.call-start = ((), (), s32[]{:S(2)}) async-start(), calls=%async_computation.16 | async-start | bytes 1216512 | tf_op jit(solution)/shard_map/all_gather | solution.py:181
  157.5 306.3 %all-gather.25.cloned.1.call-start = ((), (), s32[]{:S(2)}) async-start(), calls=%async_computation.17 | async-start | bytes 1216512 | tf_op jit(solution)/shard_map/all_gather | solution.py:183
  158.1 370.9 %all-gather.27.cloned.1.call-start = ((), (), s32[]{:S(2)}) async-start(), calls=%async_computation.18 | async-start | bytes 4866048 | tf_op jit(solution)/shard_map/all_gather | solution.py:184
  158.7 435.0 %all-gather.29.cloned.1.call-start = ((), (), s32[]{:S(2)}) async-start(), calls=%async_computation.19 | async-start | bytes 4866048 | tf_op jit(solution)/shard_map/all_gather | solution.py:185
  159.3 560.2 %reduce-scatter.33.cloned.1.call-start = ((), (), s32[]{:S(2)}) async-start(), calls=%async_computation.28 | async-start | bytes 3342336
  465.7 140.5 %copy-start.6 = (f32[256,768]{1,0:T(8,128)}, f32[256,768]{1,0:T(8,128)S(1)}, u32[]{:S(2)}) copy-start(f32[256,768]{1,0:T(8,128)S(1)} %get-tuple-element.494) | copy-start | bytes 2359300
  465.8 140.5 %copy-start.41 = (f32[256]{0:T(256)}, f32[256]{0:T(256)S(1)}, u32[]{:S(2)}) copy-start(f32[256]{0:T(256)S(1)} %broadcast_multiply_fusion.1) | copy-start | bytes 3076
  654.7 223.5 %reduce-scatter.19.cloned.1.call-start = ((), (), s32[]{:S(2)}) async-start(), calls=%async_computation.20 | async-start | bytes 13369344 | tf_op jit(solution)/shard_map/reduce_scatter | solution.py:352
  693.5 226.3 %all-gather.31.cloned.1.call-start = ((), (), s32[]{:S(2)}) async-start(), calls=%async_computation.21 | async-start | bytes 1671168 | tf_op jit(solution)/shard_map/all_gather | solution.py:329
  722.8 301.1 %reduce-scatter.21.cloned.1.call-start = ((), (), s32[]{:S(2)}) async-start(), calls=%async_computation.22 | async-start | bytes 2433024 | tf_op jit(solution)/shard_map/reduce_scatter | solution.py:378
  724.7 403.5 %reduce-scatter.23.cloned.1.call-start = ((), (), s32[]{:S(2)}) async-start(), calls=%async_computation.23 | async-start | bytes 2433024 | tf_op jit(solution)/shard_map/reduce_scatter | solution.py:379
  727.0 505.8 %reduce-scatter.27.cloned.1.call-start = ((), (), s32[]{:S(2)}) async-start(), calls=%async_computation.25 | async-start | bytes 2433024 | tf_op jit(solution)/shard_map/reduce_scatter | solution.py:381
  728.9 616.5 %reduce-scatter.25.cloned.1.call-start = ((), (), s32[]{:S(2)}) async-start(), calls=%async_computation.24 | async-start | bytes 4866048 | tf_op jit(solution)/shard_map/reduce_scatter | solution.py:380
  732.0 755.1 %reduce-scatter.29.cloned.1.call-start = ((), (), s32[]{:S(2)}) async-start(), calls=%async_computation.26 | async-start | bytes 9732096 | tf_op jit(solution)/shard_map/reduce_scatter | solution.py:382
  739.8 888.8 %reduce-scatter.31.cloned.1.call-start = ((), (), s32[]{:S(2)}) async-start(), calls=%async_computation.27 | async-start | bytes 9732096 | tf_op jit(solution)/shard_map/reduce_scatter | solution.py:383
  747.2 1006.1 %reduce-scatter.35.cloned.1.call-start = ((), (), s32[]{:S(2)}) async-start(), calls=%async_computation.29 | async-start | bytes 7299072
  964.0 789.3 %copy-start.1 = (bf16[1,512,768]{2,1,0:T(8,128)(2,1)S(1)}, bf16[1,512,768]{2,1,0:T(8,128)(2,1)}, u32[]{:S(2)}) copy-start(bf16[1,512,768]{2,1,0:T(8,128)(2,1)} %param.22) | copy-start | bytes 2359300
  (85 other events, 1709.6 us)
Sparse Core Ops, SparseCore 0:
  13.1 64.3 reduce-scatter.16
  654.9 64.5 reduce-scatter.32
  723.5 154.6 reduce-scatter.18
  880.9 38.8 all-gather.30
  925.5 98.2 reduce-scatter.20
  1029.6 98.6 reduce-scatter.22
  1134.1 98.6 reduce-scatter.26
  1238.8 106.5 reduce-scatter.24
  1351.9 135.1 reduce-scatter.28
  1493.4 135.1 reduce-scatter.30
  1634.8 118.4 reduce-scatter.34
Sparse Core Ops, SparseCore 1:
  14.8 61.0 all-gather.18
  78.6 59.3 all-gather.12
  151.9 43.4 all-gather.20
  198.2 98.6 all-gather.14
  299.8 52.3 all-gather.16
  355.1 52.9 all-gather.22
  410.9 52.9 all-gather.24
  466.6 62.3 all-gather.26
  531.8 61.8 all-gather.28
where the time goes:
time: 1770 us; the launch traced here: 1760 us
  waiting for transfers between devices  1320 us (75%)
  blocking collectives  174 us (10%)
  matrix products  142 us (8%)
  local copies, waits for them, and re-layouts  75.9 us (4%)
  other arithmetic  32.5 us (2%)
  between operations  17.9 us (1%)
    unnamed x22, waiting for transfers between devices  155 us
    reduce_scatter x1, waiting for transfers between devices, body(): lax.psum_scatter(grad_ffnin, ('seq', 'batch'), scatter_dimension=0, tiled...  142 us
    reduce_scatter x1, waiting for transfers between devices, body(): lax.psum_scatter(grad_ffnout, ('seq', 'batch'), scatter_dimension=0, tile...  142 us
    reduce_scatter x1, waiting for transfers between devices, body(): lax.psum_scatter(dkey_all.astype(jnp.bfloat16), 'seq', scatter_dimension=...  131 us
    reduce_scatter x1, waiting for transfers between devices, body(): lax.psum_scatter(grad_crosskv, ('seq', 'batch'), scatter_dimension=0, til...  113 us
    reduce_scatter x1, waiting for transfers between devices, body(): lax.psum_scatter(grad_crossout, ('seq', 'batch'), scatter_dimension=0, ti...  105 us
    reduce_scatter x1, waiting for transfers between devices, body(): lax.psum_scatter(grad_crossq, ('seq', 'batch'), scatter_dimension=0, tile...  104 us
    all_gather x1, waiting for transfers between devices, body(): keyval_all = lax.all_gather(keyval, 'seq', axis=0, tiled=True)  94.1 us
  transfers between devices with their start and end apart: 20, of which 17 were waited for; matrix products, arithmetic and copies ran while one was open for 10% of the time, Pallas kernels for 0%

commit v1 on v0

v1 whole, which is shorter than its diff:
```python
import functools

import jax
import jax.numpy as jnp
from jax import lax
from jax.experimental import pallas as pl
from jax.experimental.pallas import tpu as pltpu
from jax.sharding import PartitionSpec as P

HEADS = 12
HEAD_DIM = 64
BANK_BLOCK = 128
GROUPS = 4
GROUP_HEADS = HEADS // GROUPS
GROUP_WIDTH = GROUP_HEADS * HEAD_DIM
PACK = 640
Q01, K01, V01, Q2, K2, V2, EXTRA = 0, 128, 256, 384, 448, 512, 576
EPSILON = 1e-05
NEGATIVE = -1e30
SCALE = HEAD_DIM ** (-0.5)
LANES_IN = (((1,), (1,)), ((), ()))
ROWS_IN = (((0,), (0,)), ((), ()))
VMEM_LIMIT = 60 * 1024 * 1024


def layer_norm(values, gain, shift):
    centered = values - jnp.mean(values, axis=-1, keepdims=True)
    variance = jnp.mean(centered * centered, axis=-1, keepdims=True)
    return centered * lax.rsqrt(variance + EPSILON) * gain + shift


def gelu_exact(values):
    return jax.nn.gelu(values, approximate=False)


def rounded(values):
    return values.astype(jnp.bfloat16)


def wide(values):
    return values.astype(jnp.float32)


def matmul(left, right):
    return jnp.dot(left, right, preferred_element_type=jnp.float32)


def weight_grad(left, right):
    return lax.dot_general(left, right, ROWS_IN, preferred_element_type=jnp.float32)


def back_matmul(left, right):
    return lax.dot_general(left, right, LANES_IN, preferred_element_type=jnp.float32)


def column_sums(values):
    return jnp.sum(wide(values), axis=0)


class Grid:
    def __init__(self, mesh):
        self.seq = mesh.shape["seq"]
        self.y = mesh.shape["batch"]
        self.z = GROUPS
        self.c = 2
        self.x = self.seq // (self.z * self.c)

    def coords(self, index):
        spot, y = divmod(index, self.y)
        spot, c = divmod(spot, self.c)
        z, x = divmod(spot, self.x)
        return z, x, c, y

    def index(self, z, x, c, y):
        return ((z * self.x + x) * self.c + c) * self.y + y

    def permute(self, array, target):
        pairs = []
        for index in range(self.seq * self.y):
            pairs.append((index, self.index(*target(*self.coords(index)))))
        return lax.ppermute(array, ("seq", "batch"), pairs)

    def send(self, array, axis, shift):
        size = getattr(self, axis)
        place = "zxcy".index(axis)

        def target(*spot):
            moved = list(spot)
            moved[place] = (moved[place] + shift) % size
            return tuple(moved)

        return self.permute(array, target)

    def fold(self, z, x, c, shift):
        if shift % 2 == 0:
            return z, x, c
        return z, self.x - 1 - x, self.c - 1 - c


def roll_pieces(pieces, me, axis=0):
    count = len(pieces)
    both = jnp.stack(list(pieces) + list(pieces[:-1]), axis=axis)
    return lax.dynamic_slice_in_dim(both, (count - me) % count, count, axis)


def take(array, index, axis):
    return lax.dynamic_index_in_dim(array, index, axis, keepdims=False)


def query_parts(block):
    lane = lax.broadcasted_iota(jnp.int32, (block.shape[0], 128), 1)
    first = wide(block[:, Q01 : Q01 + 128]) * SCALE
    third = pltpu.roll(wide(block[:, Q2 : Q2 + 128]) * SCALE, 64, 1)
    return (
        rounded(jnp.where(lane < 64, first, 0.0)),
        rounded(jnp.where(lane >= 64, first, 0.0)),
        rounded(jnp.where(lane >= 64, third, 0.0)),
    )


def key_tiles(ref, start, size):
    rows = pl.ds(start, size)
    pair_keys = ref[rows, K01 : K01 + 128]
    pair_values = ref[rows, V01 : V01 + 128]
    return (
        (pair_keys, pair_keys, ref[rows, Q2 : Q2 + 128]),
        (pair_values, pair_values, ref[rows, V2 : V2 + 128]),
    )


def allowed_keys(key_first, query_first, prefix_len, shape):
    key_pos = key_first + lax.broadcasted_iota(jnp.int32, shape, 0)
    query_pos = query_first + lax.broadcasted_iota(jnp.int32, shape, 1)
    return (key_pos <= query_pos) | (key_pos < prefix_len)


def each_block(table, refs, rows, query_first, prefix_len, work):
    half = refs[0].shape[0] // rows
    for part, ref in enumerate(refs):

        def step(local, carry, part=part, ref=ref):
            block = part * half + local
            key_first = table[block]
            last = key_first + rows - 1
            seen = (key_first <= query_first + rows - 1) | (key_first < prefix_len)
            whole = (last <= query_first) | (last < prefix_len)

            @pl.when(seen & whole)
            def _():
                work(ref, local * rows, block, key_first, False)

            @pl.when(seen & jnp.logical_not(whole))
            def _():
                work(ref, local * rows, block, key_first, True)

            return carry

        lax.fori_loop(0, half, step, 0)


def forward_kernel(rows, blocks, table, own, other, out, lse, query, accum, stats):
    m = pl.program_id(0)
    half = blocks // 2
    block = table[blocks + m]
    query_first = table[blocks + GROUPS + m]
    prefix_len = table[blocks + 2 * GROUPS]

    def load(ref, local):
        for head, part in enumerate(query_parts(ref[pl.ds(local * rows, rows), :])):
            query[head] = part

    @pl.when(block < half)
    def _():
        load(own, block)

    @pl.when(block >= half)
    def _():
        load(other, block - half)

    accum[...] = jnp.zeros_like(accum)
    stats[0:8, :] = jnp.full((8, rows), NEGATIVE, jnp.float32)
    stats[8:16, :] = jnp.zeros((8, rows), jnp.float32)

    def work(ref, start, block, key_first, masked):
        keys, values = key_tiles(ref, start, rows)
        if masked:
            mask = allowed_keys(key_first, query_first, prefix_len, (rows, rows))
        for head in range(GROUP_HEADS):
            scores = lax.dot_general(
                keys[head], query[head], LANES_IN, preferred_element_type=jnp.float32
            )
            if masked:
                scores = jnp.where(mask, scores, NEGATIVE)
            old = stats[head : head + 1, :]
            top = jnp.maximum(old, jnp.max(scores, axis=0, keepdims=True))
            weights = jnp.exp(scores - top)
            shrink = jnp.exp(old - top)
            stats[head : head + 1, :] = top
            stats[8 + head : 9 + head, :] = stats[8 + head : 9 + head, :] * shrink + jnp.sum(
                weights, axis=0, keepdims=True
            )
            accum[head] = accum[head] * shrink + lax.dot_general(
                values[head], rounded(weights), ROWS_IN, preferred_element_type=jnp.float32
            )

    each_block(table, (own, other), rows, query_first, prefix_len, work)
    totals = stats[8 : 8 + GROUP_HEADS, :]
    final = [accum[head] / totals[head : head + 1, :] for head in range(GROUP_HEADS)]
    line = lax.broadcasted_iota(jnp.int32, (128, rows), 0)
    out[0, :, 0:128] = jnp.where(line < 64, final[0], final[1]).T
    out[0, :, 128:256] = jnp.where(line < 64, final[2], 0.0).T
    lse[0] = jnp.zeros((8, rows), jnp.float32)
    lse[0, 0:GROUP_HEADS, :] = stats[0:GROUP_HEADS, :] + jnp.log(totals)


def backward_kernel(
    rows, blocks, table, own, other, dout, out, lse, own_grad, other_grad, query, accum, qgrad
):
    m = pl.program_id(0)
    half = blocks // 2
    block = table[blocks + m]
    query_first = table[blocks + GROUPS + m]
    prefix_len = table[blocks + 2 * GROUPS]

    @pl.when(m == 0)
    def _():
        def clear(index, carry):
            accum[pl.ds(index * rows, rows), :] = jnp.zeros((rows, PACK), jnp.float32)
            return carry

        lax.fori_loop(0, blocks, clear, 0)

    def load(ref, local):
        for head, part in enumerate(query_parts(ref[pl.ds(local * rows, rows), :])):
            query[head] = part

    @pl.when(block < half)
    def _():
        load(own, block)

    @pl.when(block >= half)
    def _():
        load(other, block - half)

    lane = lax.broadcasted_iota(jnp.int32, (rows, 128), 1)
    pair = wide(dout[0, :, 0:128])
    third = wide(dout[0, :, 128:256])
    query[3] = rounded(jnp.where(lane < 64, pair, 0.0))
    query[4] = rounded(jnp.where(lane >= 64, pair, 0.0))
    query[5] = rounded(jnp.where(lane < 64, third, 0.0))
    pair_prod = (pair * out[0, :, 0:128]).T
    third_prod = (third * out[0, :, 128:256]).T
    deltas = (
        jnp.sum(pair_prod[0:64], axis=0, keepdims=True),
        jnp.sum(pair_prod[64:128], axis=0, keepdims=True),
        jnp.sum(third_prod[0:64], axis=0, keepdims=True),
    )
    for head in range(GROUP_HEADS):
        qgrad[GROUP_HEADS, head : head + 1, :] = deltas[head]
        qgrad[head] = jnp.zeros((128, rows), jnp.float32)

    def work(ref, start, block, key_first, masked):
        keys, values = key_tiles(ref, start, rows)
        if masked:
            mask = allowed_keys(key_first, query_first, prefix_len, (rows, rows))
        key_parts, value_parts = [], []
        for head in range(GROUP_HEADS):
            scores = lax.dot_general(
                keys[head], query[head], LANES_IN, preferred_element_type=jnp.float32
            )
            if masked:
                scores = jnp.where(mask, scores, NEGATIVE)
            probs = jnp.exp(scores - lse[0, head : head + 1, :])
            grads = lax.dot_general(
                values[head], query[3 + head], LANES_IN, preferred_element_type=jnp.float32
            )
            low = rounded(probs * (grads - qgrad[GROUP_HEADS, head : head + 1, :]))
            value_parts.append(matmul(rounded(probs), query[3 + head]))
            key_parts.append(matmul(low, query[head]))
            qgrad[head] += lax.dot_general(
                keys[head], low, ROWS_IN, preferred_element_type=jnp.float32
            )
        span = pl.ds(pl.multiple_of(block * rows, rows), rows)
        accum[span, K01 : K01 + 128] += key_parts[0] + key_parts[1]
        accum[span, V01 : V01 + 128] += value_parts[0] + value_parts[1]
        accum[span, Q2 : Q2 + 128] += key_parts[2]
        accum[span, V2 : V2 + 128] += value_parts[2]

    each_block(table, (own, other), rows, query_first, prefix_len, work)
    line = lax.broadcasted_iota(jnp.int32, (128, rows), 0)
    span = pl.ds(pl.multiple_of(block * rows, rows), rows)
    accum[span, Q01 : Q01 + 128] = jnp.where(line < 64, qgrad[0], qgrad[1]).T * SCALE
    moved = pltpu.roll(jnp.where(line >= 64, qgrad[2], 0.0).T * SCALE, 64, 1)
    accum[span, Q2 : Q2 + 128] += moved

    @pl.when(m == GROUPS - 1)
    def _():
        def write(index, carry):
            source = pl.ds(index * rows, rows)
            own_grad[source, :] = rounded(accum[source, :])
            other_grad[source, :] = rounded(accum[pl.ds((half + index) * rows, rows), :])
            return carry

        lax.fori_loop(0, half, write, 0)


def whole(shape):
    return pl.BlockSpec(shape, lambda *_: (0,) * len(shape), pipeline_mode=pl.Buffered(1))


def slab(shape):
    return pl.BlockSpec((1,) + shape, lambda m, *_: (m, 0, 0))


def self_forward(table, own, other, rows):
    half, _ = own.shape
    blocks = 2 * half // rows
    pairs = GROUPS * blocks * GROUP_HEADS // 2
    return pl.pallas_call(
        functools.partial(forward_kernel, rows, blocks),
        grid_spec=pltpu.PrefetchScalarGridSpec(
            num_scalar_prefetch=1,
            grid=(GROUPS,),
            in_specs=[whole((half, PACK)), whole((half, PACK))],
            out_specs=[slab((rows, 256)), slab((8, rows))],
            scratch_shapes=[
                pltpu.VMEM((GROUP_HEADS, rows, 128), jnp.bfloat16),
                pltpu.VMEM((GROUP_HEADS, 128, rows), jnp.float32),
                pltpu.VMEM((16, rows), jnp.float32),
            ],
        ),
        out_shape=[
            jax.ShapeDtypeStruct((GROUPS, rows, 256), jnp.float32),
            jax.ShapeDtypeStruct((GROUPS, 8, rows), jnp.float32),
        ],
        compiler_params=pltpu.CompilerParams(vmem_limit_bytes=VMEM_LIMIT),
        cost_estimate=pl.CostEstimate(
            flops=pairs * rows * rows * 128 * 4,
            bytes_accessed=4 * half * PACK,
            transcendentals=pairs * rows * rows,
        ),
        name="self_forward",
    )(table, own, other)


def self_backward(table, own, other, dout, out, lse, rows):
    half, _ = own.shape
    blocks = 2 * half // rows
    pairs = GROUPS * blocks * GROUP_HEADS // 2
    return pl.pallas_call(
        functools.partial(backward_kernel, rows, blocks),
        grid_spec=pltpu.PrefetchScalarGridSpec(
            num_scalar_prefetch=1,
            grid=(GROUPS,),
            in_specs=[
                whole((half, PACK)),
                whole((half, PACK)),
                slab((rows, 256)),
                slab((rows, 256)),
                slab((8, rows)),
            ],
            out_specs=[whole((half, PACK)), whole((half, PACK))],
            scratch_shapes=[
                pltpu.VMEM((2 * GROUP_HEADS, rows, 128), jnp.bfloat16),
                pltpu.VMEM((2 * half, PACK), jnp.float32),
                pltpu.VMEM((GROUP_HEADS + 1, 128, rows), jnp.float32),
            ],
        ),
        out_shape=[jax.ShapeDtypeStruct((half, PACK), jnp.bfloat16)] * 2,
        compiler_params=pltpu.CompilerParams(vmem_limit_bytes=VMEM_LIMIT),
        cost_estimate=pl.CostEstimate(
            flops=pairs * rows * rows * 128 * 10,
            bytes_accessed=8 * half * PACK,
            transcendentals=pairs * rows * rows,
        ),
        name="self_backward",
    )(table, own, other, dout, out, lse)


def pair_heads(block, scale=1.0):
    lane = lax.broadcasted_iota(jnp.int32, block.shape, 1)
    values = wide(block) * scale
    return rounded(jnp.where(lane < 64, values, 0.0)), rounded(jnp.where(lane >= 64, values, 0.0))


def cross_forward_kernel(query, keys, values, out, lse):
    rows = query.shape[0]
    parts = pair_heads(query[...], SCALE)
    sides = []
    lse[0] = jnp.zeros((8, rows), jnp.float32)
    for head in range(2):
        scores = lax.dot_general(
            keys[...], parts[head], LANES_IN, preferred_element_type=jnp.float32
        )
        top = jnp.max(scores, axis=0, keepdims=True)
        weights = jnp.exp(scores - top)
        total = jnp.sum(weights, axis=0, keepdims=True)
        mixed = lax.dot_general(
            values[...], rounded(weights), ROWS_IN, preferred_element_type=jnp.float32
        )
        sides.append(mixed / total)
        lse[0, head : head + 1, :] = top + jnp.log(total)
    line = lax.broadcasted_iota(jnp.int32, (128, rows), 0)
    out[...] = rounded(jnp.where(line < 64, sides[0], sides[1]).T)


def cross_backward_kernel(query, keys, values, dout, lse, qgrad, kgrad, vgrad):
    rows = query.shape[0]
    parts = pair_heads(query[...], SCALE)
    grads = pair_heads(dout[...])
    sides, key_parts, value_parts = [], [], []
    for head in range(2):
        scores = lax.dot_general(
            keys[...], parts[head], LANES_IN, preferred_element_type=jnp.float32
        )
        probs = jnp.exp(scores - lse[0, head : head + 1, :])
        slopes = lax.dot_general(
            values[...], grads[head], LANES_IN, preferred_element_type=jnp.float32
        )
        delta = jnp.sum(probs * slopes, axis=0, keepdims=True)
        low = rounded(probs * (slopes - delta))
        value_parts.append(matmul(rounded(probs), grads[head]))
        key_parts.append(matmul(low, parts[head]))
        sides.append(lax.dot_general(keys[...], low, ROWS_IN, preferred_element_type=jnp.float32))
    line = lax.broadcasted_iota(jnp.int32, (128, rows), 0)
    qgrad[...] = rounded(jnp.where(line < 64, sides[0], sides[1]).T * SCALE)
    kgrad[...] = rounded(key_parts[0] + key_parts[1])
    vgrad[...] = rounded(value_parts[0] + value_parts[1])


def cross_forward(query, pair):
    rows, width = query.shape
    count = width // 128
    kept = pair.shape[0]
    return pl.pallas_call(
        cross_forward_kernel,
        grid=(count,),
        in_specs=[
            pl.BlockSpec((rows, 128), lambda i: (0, i)),
            pl.BlockSpec((kept, 128), lambda i: (0, i)),
            pl.BlockSpec((kept, 128), lambda i: (0, count + i)),
        ],
        out_specs=[
            pl.BlockSpec((rows, 128), lambda i: (0, i)),
            pl.BlockSpec((1, 8, rows), lambda i: (i, 0, 0)),
        ],
        out_shape=[
            jax.ShapeDtypeStruct((rows, width), jnp.bfloat16),
            jax.ShapeDtypeStruct((count, 8, rows), jnp.float32),
        ],
        compiler_params=pltpu.CompilerParams(vmem_limit_bytes=VMEM_LIMIT),
        cost_estimate=pl.CostEstimate(
            flops=8 * rows * kept * width, bytes_accessed=4 * kept * width, transcendentals=12 * rows * kept
        ),
        name="cross_forward",
    )(query, pair, pair)


def cross_backward(query, pair, dout, lse):
    rows, width = query.shape
    count = width // 128
    kept = pair.shape[0]
    return pl.pallas_call(
        cross_backward_kernel,
        grid=(count,),
        in_specs=[
            pl.BlockSpec((rows, 128), lambda i: (0, i)),
            pl.BlockSpec((kept, 128), lambda i: (0, i)),
            pl.BlockSpec((kept, 128), lambda i: (0, count + i)),
            pl.BlockSpec((rows, 128), lambda i: (0, i)),
            pl.BlockSpec((1, 8, rows), lambda i: (i, 0, 0)),
        ],
        out_specs=[
            pl.BlockSpec((rows, 128), lambda i: (0, i)),
            pl.BlockSpec((kept, 128), lambda i: (0, i)),
            pl.BlockSpec((kept, 128), lambda i: (0, i)),
        ],
        out_shape=[
            jax.ShapeDtypeStruct((rows, width), jnp.bfloat16),
            jax.ShapeDtypeStruct((kept, width), jnp.bfloat16),
            jax.ShapeDtypeStruct((kept, width), jnp.bfloat16),
        ],
        compiler_params=pltpu.CompilerParams(vmem_limit_bytes=VMEM_LIMIT),
        cost_estimate=pl.CostEstimate(
            flops=20 * rows * kept * width, bytes_accessed=8 * kept * width, transcendentals=12 * rows * kept
        ),
        name="cross_backward",
    )(query, pair, pair, dout, lse)


def pick_kernel(table, bank, out):
    i = pl.program_id(0)
    keep = table[pl.num_programs(0) + i]
    out[0] = jnp.where(keep > 0, bank[0], jnp.zeros_like(bank[0]))


def pick_rows(chunks, spots, found):
    count = spots.shape[0]
    size = chunks.shape[1:]
    table = jnp.concatenate([spots, found.astype(jnp.int32)])
    return pl.pallas_call(
        pick_kernel,
        grid_spec=pltpu.PrefetchScalarGridSpec(
            num_scalar_prefetch=1,
            grid=(count,),
            in_specs=[pl.BlockSpec((1,) + size, lambda i, t: (t[i], 0, 0))],
            out_specs=pl.BlockSpec((1,) + size, lambda i, t: (i, 0, 0)),
        ),
        out_shape=jax.ShapeDtypeStruct((count,) + size, chunks.dtype),
        name="pick_rows",
    )(table, chunks)


def place_kernel(count, table, grads, out):
    spot = pl.program_id(0)
    out[...] = jnp.zeros_like(out)
    for i in range(count):

        @pl.when(table[i] == spot)
        def _(i=i):
            out[0] += wide(grads[i])


def place_rows(grads, spots, chunks):
    count = spots.shape[0]
    size = grads.shape[1:]
    return pl.pallas_call(
        functools.partial(place_kernel, count),
        grid_spec=pltpu.PrefetchScalarGridSpec(
            num_scalar_prefetch=1,
            grid=(chunks,),
            in_specs=[whole((count,) + size)],
            out_specs=pl.BlockSpec((1,) + size, lambda n, t: (n, 0, 0)),
        ),
        out_shape=jax.ShapeDtypeStruct((chunks,) + size, jnp.float32),
        name="place_rows",
    )(spots, grads)


def scatter_step(grid, array, axis, me, place):
    size = getattr(grid, axis)
    total = wide(take(array, me, place))
    for shift in range(1, size):
        piece = take(array, (me + shift) % size, place)
        total = total + wide(grid.send(piece, axis, shift))
    return rounded(total)


def body(
    grid,
    tokens,
    cotangent,
    bank,
    prefix,
    blocks,
    self_qkv,
    self_out,
    cross_q,
    cross_kv,
    cross_out,
    ffn_in,
    ffn_out,
    gains,
    biases,
):
    Z, X, C, Y = grid.z, grid.x, grid.c, grid.y
    devices = grid.seq * Y
    seq_index = lax.axis_index("seq")
    my_y = lax.axis_index("batch")
    my_c = seq_index % C
    my_x = (seq_index // C) % X
    my_z = seq_index // (C * X)
    rows, width = tokens.shape[1:]
    hidden = ffn_in.shape[1]
    part = width // devices
    fan = hidden // width
    inputs = tokens[0]

    small = jnp.concatenate([gains, biases], axis=0).T
    small = jnp.pad(small, ((0, 0), (0, 128 - small.shape[1])))
    first_pack = jnp.concatenate([self_out, cross_q, cross_out, cross_kv, small], axis=1)
    outer_blocks = ffn_out.reshape(fan, part, width).transpose(1, 0, 2).reshape(part, hidden)
    second_pack = jnp.concatenate([ffn_in, outer_blocks], axis=1)
    first_all = lax.all_gather(first_pack, ("seq", "batch"), axis=0, tiled=True)
    second_all = lax.all_gather(second_pack, ("seq", "batch"), axis=0, tiled=True)

    token_parts = [inputs] + [grid.send(inputs, "z", m) for m in range(1, Z)]

    grouped = self_qkv.reshape(part, 3, GROUPS, GROUP_WIDTH)
    extra = jnp.stack([biases[3], biases[4]], axis=1)
    extra = jnp.broadcast_to(
        jnp.pad(extra, ((0, 0), (0, PACK - EXTRA - 2)))[:, None], (part, GROUPS, PACK - EXTRA)
    )
    packed = jnp.concatenate(
        [
            grouped[:, 0, :, :128],
            grouped[:, 1, :, :128],
            grouped[:, 2, :, :128],
            grouped[:, 0, :, 128:],
            grouped[:, 1, :, 128:],
            grouped[:, 2, :, 128:],
            extra,
        ],
        axis=2,
    ).transpose(1, 0, 2)
    pieces = [take(packed, my_z, 0)]
    for shift in range(1, Z):
        pieces.append(grid.send(take(packed, (my_z + shift) % Z, 0), "z", shift))
    gathered = roll_pieces([pieces[(-m) % Z] for m in range(Z)], my_z)
    for axis, me in (("y", my_y), ("x", my_x), ("c", my_c)):
        size = getattr(grid, axis)
        pieces = [gathered] + [grid.send(gathered, axis, m) for m in range(1, size)]
        gathered = roll_pieces([pieces[(-m) % size] for m in range(size)], me)
    qkv_group = gathered.transpose(3, 1, 0, 2, 4, 5).reshape(width, PACK)
    column = jnp.arange(PACK)
    bias_rows = lax.dynamic_slice_in_dim(qkv_group[:, EXTRA : EXTRA + 2], my_z * GROUP_WIDTH, GROUP_WIDTH, 0)
    query_bias, value_bias = bias_rows[:, 0], bias_rows[:, 1]
    none = jnp.zeros((128,), jnp.bfloat16)
    qkv_bias = wide(
        jnp.concatenate(
            [query_bias[:128], none, value_bias[:128], query_bias[128:], none[:64], value_bias[128:], none[:64]]
        )
    )
    real = (column < EXTRA)[None]
    qkv_weight = jnp.where(real, qkv_group, jnp.zeros_like(qkv_group))

    chunk = BANK_BLOCK * blocks.shape[1] // grid.seq
    per_block = BANK_BLOCK // chunk
    local_chunks = bank.shape[1] // chunk
    local_blocks = bank.shape[1] // BANK_BLOCK
    bank_chunks = bank[0].reshape(local_chunks, chunk, width)
    home = seq_index * local_blocks
    every = jnp.arange(grid.seq, dtype=jnp.int32)
    wanted = jnp.take(blocks[0], every // per_block) - home
    found = (wanted >= 0) & (wanted < local_blocks)
    spots = jnp.where(found, wanted * per_block + every % per_block, 0)
    picked = pick_rows(bank_chunks, spots, found).reshape(Z, X, C, chunk, width)
    shares = scatter_step(grid, picked, "c", my_c, 2)
    shares = scatter_step(grid, shares, "x", my_x, 1)
    own_rows = scatter_step(grid, shares, "z", my_z, 0)

    def spread(own):
        array = jnp.stack([own] + [grid.send(own, "z", m) for m in range(1, Z)])
        array = jnp.stack([array] + [grid.send(array, "x", m) for m in range(1, X)])
        return jnp.stack([array, grid.send(array, "c", 1)])

    all_rows = spread(own_rows).reshape(grid.seq * chunk, width)

    qkv_parts = [rounded(matmul(piece, qkv_weight) + qkv_bias) for piece in token_parts]
    own_side = jnp.concatenate(
        qkv_parts + [grid.send(piece, "x", m) for m in range(1, X) for piece in qkv_parts], axis=0
    )
    other_side = grid.send(own_side, "c", 1)

    order = jnp.arange(C * X * Z, dtype=jnp.int32)
    block_z = (my_z - order % Z) % Z
    block_x = (my_x - (order // Z) % X) % X
    block_c = (my_c + order // (Z * X)) % C
    key_firsts = ((block_z * X + block_x) * C + block_c) * rows
    turn = jnp.arange(GROUPS, dtype=jnp.int32)
    mirror_x = (2 * my_x - X + 1) % X
    query_blocks = jnp.where(turn % 2 == 0, turn, (X + mirror_x) * Z + turn)
    query_firsts = jnp.take(key_firsts, query_blocks)
    table = jnp.concatenate([key_firsts, query_blocks, query_firsts, prefix]).astype(jnp.int32)

    attention, lse = self_forward(table, own_side, other_side, rows)
    attention_mine = rounded(attention)

    def to_owner(array, m):
        def target(z, x, c, y):
            z, x, c = grid.fold((z - m) % Z, x, c, m)
            return z, x, c, y

        return grid.permute(array, target)

    def to_worker(array, m):
        def target(z, x, c, y):
            z, x, c = grid.fold((z + m) % Z, x, c, m)
            return z, x, c, y

        return grid.permute(array, target)

    pieces = [attention_mine[0]] + [to_owner(attention_mine[m], m) for m in range(1, Z)]
    attention_low = (
        roll_pieces(pieces, my_z)[:, :, :GROUP_WIDTH].transpose(1, 0, 2).reshape(rows, width)
    )

    selfout_full = first_all[:, :width]
    crossq_full = first_all[:, width : 2 * width]
    crossout_full = first_all[:, 2 * width : 3 * width]
    crosskv_full = first_all[:, 3 * width : 5 * width]
    small_full = wide(first_all[:, 5 * width :].T)
    gain = small_full[:3]
    bias = small_full[3:17]
    ffnin_full = second_all[:, :hidden]
    ffnout_full = (
        second_all[:, hidden:]
        .reshape(devices, part, fan, width)
        .transpose(0, 2, 1, 3)
        .reshape(hidden, width)
    )

    resid_one = wide(inputs) + matmul(attention_low, selfout_full) + bias[5]
    hidden_one = layer_norm(resid_one, gain[0], bias[0])
    hidden_one_low = rounded(hidden_one)
    cross_query = rounded(matmul(hidden_one_low, crossq_full) + bias[6])
    cross_pair = rounded(
        matmul(all_rows, crosskv_full) + jnp.concatenate([jnp.zeros((width,), jnp.float32), bias[7]])
    )
    cross_att, cross_lse = cross_forward(cross_query, cross_pair)
    resid_two = hidden_one + matmul(cross_att, crossout_full) + bias[8]
    hidden_two = layer_norm(resid_two, gain[1], bias[1])
    hidden_two_low = rounded(hidden_two)
    inner = matmul(hidden_two_low, ffnin_full) + bias[10:14].reshape(-1)
    activated = rounded(gelu_exact(inner))
    resid_three = hidden_two + matmul(activated, ffnout_full) + bias[9]
    output = layer_norm(resid_three, gain[2], bias[2])

    _unused, norm_three = jax.vjp(layer_norm, resid_three, gain[2], bias[2])
    dresid_three, dgain_three, dshift_three = norm_three(wide(cotangent[0]))
    douter_low = rounded(dresid_three)
    grad_ffnout = rounded(weight_grad(activated, douter_low))
    _unused, gelu_back = jax.vjp(gelu_exact, inner)
    dinner_low = rounded(gelu_back(back_matmul(douter_low, ffnout_full))[0])
    grad_ffnin = rounded(weight_grad(hidden_two_low, dinner_low))

    def reduce_shards(array):
        count = array.shape[0] // devices
        columns = array.shape[1]
        array = array.reshape(Z, X, C, Y, count, columns)
        array = scatter_step(grid, array, "c", my_c, 2)
        cut = columns // 256 * 128
        left = scatter_step(grid, array[..., :cut], "x", my_x, 1)
        right = scatter_step(grid, array[..., cut:], "y", my_y, 2)
        left = scatter_step(grid, left, "y", my_y, 1)
        right = scatter_step(grid, right, "x", my_x, 1)
        array = jnp.concatenate([left, right], axis=-1)
        total = wide(take(array, my_z, 0))
        for shift in range(1, Z):
            total = total + wide(grid.send(take(array, (my_z + shift) % Z, 0), "z", shift))
        return total

    out_ffnout = reduce_shards(grad_ffnout)
    out_ffnin = reduce_shards(grad_ffnin)

    _unused, norm_two = jax.vjp(layer_norm, resid_two, gain[1], bias[1])
    dresid_two, dgain_two, dshift_two = norm_two(dresid_three + back_matmul(dinner_low, ffnin_full))
    dcross_low = rounded(dresid_two)
    grad_crossout = rounded(weight_grad(cross_att, dcross_low))
    dcross_att = rounded(back_matmul(dcross_low, crossout_full))
    dcross_query, dcross_key, dcross_value = cross_backward(
        cross_query, cross_pair, dcross_att, cross_lse
    )
    grad_crossq = rounded(weight_grad(hidden_one_low, dcross_query))
    _unused, norm_one = jax.vjp(layer_norm, resid_one, gain[0], bias[0])
    dresid_one, dgain_one, dshift_one = norm_one(dresid_two + back_matmul(dcross_query, crossq_full))
    dbranch_low = rounded(dresid_one)
    grad_selfout = rounded(weight_grad(attention_low, dbranch_low))
    datt_low = rounded(back_matmul(dbranch_low, selfout_full))
    datt_groups = jnp.pad(
        datt_low.reshape(rows, GROUPS, GROUP_WIDTH).transpose(1, 0, 2),
        ((0, 0), (0, 0), (0, 256 - GROUP_WIDTH)),
    )
    pieces = [take(datt_groups, my_z, 0)]
    for m in range(1, Z):
        pieces.append(to_worker(take(datt_groups, (my_z + m) % Z, 0), m))
    own_grad, other_grad = self_backward(
        table, own_side, other_side, jnp.stack(pieces), attention, lse, rows
    )

    dcross_all = jnp.concatenate([dcross_key, dcross_value], axis=1)
    dcross_all = dcross_all.reshape(C, X, Z, chunk, 2 * width)

    def unspread(array):
        total = wide(array[0]) + wide(grid.send(array[1], "c", 1))
        array = rounded(total)
        total = wide(array[0])
        for m in range(1, X):
            total = total + wide(grid.send(array[m], "x", -m))
        array = rounded(total)
        total = wide(array[0])
        for m in range(1, Z):
            total = total + wide(grid.send(array[m], "z", -m))
        return rounded(total)

    dcross_pair = unspread(dcross_all)
    grad_crosskv = rounded(weight_grad(own_rows, dcross_pair))
    drows = spread(rounded(back_matmul(dcross_pair, crosskv_full))).reshape(grid.seq, chunk, width)
    source = (block_z * X + block_x) * C + block_c
    target = jnp.take(blocks[0], source // per_block) - home
    inside = (target >= 0) & (target < local_blocks)
    places = jnp.where(inside, target * per_block + source % per_block, -1)
    bank_grad = place_rows(drows, places, local_chunks).reshape(bank.shape[1], width)

    dqkv = rounded(wide(own_grad) + wide(grid.send(other_grad, "c", 1)))
    dqkv = dqkv.reshape(X, Z, rows, PACK)
    total = wide(dqkv[0])
    for m in range(1, X):
        total = total + wide(grid.send(dqkv[m], "x", -m))
    dqkv = rounded(total)
    dqkv = jnp.where(real[None], dqkv, jnp.zeros_like(dqkv))
    tokens_grad = dresid_one + back_matmul(dqkv[0], qkv_weight)
    for m in range(1, Z):
        tokens_grad = tokens_grad + wide(
            grid.send(rounded(back_matmul(dqkv[m], qkv_weight)), "z", -m)
        )
    grad_group = weight_grad(token_parts[0], dqkv[0])
    for m in range(1, Z):
        grad_group = grad_group + weight_grad(token_parts[m], dqkv[m])
    dqkv_sums = jnp.sum(wide(dqkv), axis=(0, 1))
    sums = jnp.stack(
        [
            jnp.concatenate([dqkv_sums[Q01 : Q01 + 128], dqkv_sums[Q2 : Q2 + 64]]),
            jnp.concatenate([dqkv_sums[V01 : V01 + 128], dqkv_sums[V2 : V2 + 64]]),
        ],
        axis=1,
    )
    sums = lax.dynamic_update_slice_in_dim(
        jnp.zeros((width, 2), jnp.float32), sums, my_z * GROUP_WIDTH, 0
    )
    grad_group = jnp.concatenate(
        [grad_group[:, :EXTRA], jnp.pad(sums, ((0, 0), (0, PACK - EXTRA - 2)))], axis=1
    )
    grad_group = rounded(grad_group).reshape(Z, X, C, Y, part, PACK)
    grad_group = scatter_step(grid, grad_group, "c", my_c, 2)
    grad_group = scatter_step(grid, grad_group, "x", my_x, 1)
    grad_group = scatter_step(grid, grad_group, "y", my_y, 1)
    pieces = [take(grad_group, my_z, 0)]
    for shift in range(1, Z):
        pieces.append(grid.send(take(grad_group, (my_z + shift) % Z, 0), "z", shift))
    grad_groups = wide(roll_pieces([pieces[(-m) % Z] for m in range(Z)], my_z))
    pair = grad_groups[:, :, :384].reshape(GROUPS, part, 3, 128)
    last = grad_groups[:, :, 384:576].reshape(GROUPS, part, 3, 64)
    out_qkv = (
        jnp.concatenate([pair, last], axis=-1).transpose(1, 2, 0, 3).reshape(part, 3 * width)
    )
    late_bias = jnp.sum(grad_groups[:, :, EXTRA : EXTRA + 2], axis=0)

    bias_rows = jnp.stack(
        [
            dgain_one,
            dgain_two,
            dgain_three,
            dshift_one,
            dshift_two,
            dshift_three,
            column_sums(dbranch_low),
            column_sums(dcross_query),
            column_sums(dcross_pair[:, width:]),
            column_sums(dcross_low),
            column_sums(douter_low),
        ]
    )
    bias_rows = jnp.concatenate([bias_rows, column_sums(dinner_low).reshape(fan, width)], axis=0)
    bias_columns = jnp.pad(rounded(bias_rows.T), ((0, 0), (0, 128 - bias_rows.shape[0])))
    rest = jnp.concatenate(
        [grad_selfout, grad_crossq, grad_crossout, grad_crosskv, bias_columns], axis=1
    )
    out_rest = reduce_shards(rest)
    out_small = out_rest[:, 5 * width :].T
    bias_grad = jnp.concatenate([out_small[3:6], late_bias.T, out_small[6:15]], axis=0)
    return (
        rounded(output)[None],
        tokens_grad[None],
        bank_grad[None],
        out_qkv,
        out_rest[:, :width],
        out_rest[:, width : 2 * width],
        out_rest[:, 3 * width : 5 * width],
        out_rest[:, 2 * width : 3 * width],
        out_ffnin,
        out_ffnout,
        out_small[:3],
        bias_grad,
    )


def solution(mesh):
    split = P("batch", "seq", None)
    shard = P(("seq", "batch"), None)
    flat = P(None, ("seq", "batch"))
    return jax.shard_map(
        functools.partial(body, Grid(mesh)),
        mesh=mesh,
        in_specs=(split, split, split, P("batch"), P("batch", None)) + (shard,) * 7 + (flat, flat),
        out_specs=(split, split, split) + (shard,) * 7 + (flat, flat),
        check_vma=False,
    )
```

time: 1770 us -> 719 us (0.41)
  waiting for transfers between devices: 1320 us -> 252 us
  blocking collectives: 174 us -> 0 us
  Pallas kernels: 0 us -> 125 us
  starting transfers between devices: 0.83 us -> 99 us
  matrix products: 142 us -> 71.3 us
  local copies, waits for them, and re-layouts: 75.9 us -> 97.7 us
    reduce_scatter x8 -> x0, waiting for transfers between devices: 791 us -> none  [the longest x1 142 us: body(): lax.psum_scatter(grad_ffnin, ('seq', 'batch'), scatter_dimension=0, tiled...]
    all_gather x10 -> x2, waiting for transfers between devices: 371 us -> 0.04 us  [the longest x1 0.02 us: body(): first_all = lax.all_gather(first_pack, ('seq', 'batch'), axis=0, tiled=True)]
    ppermute x0 -> x75, waiting for transfers between devices: none -> 252 us  [permute(): return lax.ppermute(array, ('seq', 'batch'), pairs)]
    unnamed x22 -> x2, waiting for transfers between devices: 155 us -> 0.03 us
    all_gather x2 -> x0, blocking collectives: 135 us -> none  [the longest x1 71.1 us: body(): lax.all_gather(biases, ('seq', 'batch'), axis=1, tiled=True)]
    pallas_call x0 -> x6, Pallas kernels: none -> 125 us  [the longest x1 44.5 us: self_backward(): pl.pallas_call(functools.partial(backward_kernel, rows, blocks), grid_spe...]
    ppermute x0 -> x75, starting transfers between devices: none -> 98.9 us  [permute(): return lax.ppermute(array, ('seq', 'batch'), pairs)]
    dot_general x42 -> x20, matrix products: 104 us -> 41.2 us  [the longest x10 21.3 us: weight_grad(): lax.dot_general(left, right, ROWS_IN, preferred_element_type=jnp.float32)]
  transfers between devices with their start and end apart: 20 -> 77, of which waited for: 17 -> 37; matrix products, arithmetic and copies ran while one was open for 10% -> 19% of each run, Pallas kernels for 0% -> 16%
where the time goes in v1:
time: 719 us; the launch traced here: 707 us
  waiting for transfers between devices  252 us (35%)
  Pallas kernels  125 us (17%)
  starting transfers between devices  99 us (14%)
  local copies, waits for them, and re-layouts  97.7 us (14%)
  matrix products  71.3 us (10%)
  other arithmetic  44.7 us (6%)
  between operations  16.7 us (2%)
    ppermute x75, waiting for transfers between devices, permute(): return lax.ppermute(array, ('seq', 'batch'), pairs)  252 us
    ppermute x75, starting transfers between devices, permute(): return lax.ppermute(array, ('seq', 'batch'), pairs)  98.9 us
    pallas_call x1, Pallas kernels, self_backward(): pl.pallas_call(functools.partial(backward_kernel, rows, blocks), grid_spe...  44.5 us
    pallas_call x1, Pallas kernels, self_forward(): pl.pallas_call(functools.partial(forward_kernel, rows, blocks), grid_spec...  42.7 us
    dot_general x10, matrix products, matmul(): return jnp.dot(left, right, preferred_element_type=jnp.float32)  30.1 us
    dot_general x10, matrix products, weight_grad(): lax.dot_general(left, right, ROWS_IN, preferred_element_type=jnp.float32)  21.3 us
    convert_element_type x26, other arithmetic, rounded(): return values.astype(jnp.bfloat16)  20.2 us
    dot_general x10, matrix products, back_matmul(): lax.dot_general(left, right, LANES_IN, preferred_element_type=jnp.float32)  19.8 us
  transfers between devices with their start and end apart: 77, of which 37 were waited for; matrix products, arithmetic and copies ran while one was open for 19% of the time, Pallas kernels for 16%

profile of v1, /device:TPU:0, one launch (start us, length us, event | category | flops | bytes accessed | tf_op | source)
XLA Modules:
  0.0 706.9 jit_solution(5470517746435428536)
XLA Ops:
  27.8 20.4 %collective-permute-done = bf16[24,640]{1,0:T(8,128)(2,1)S(1)} collective-permute-done((bf16[24,640]{1,0:T(8,128)(2,1)S(1)}, bf16[24,640]{1,0:T(8,128)(2,1)S(1)}, u32[]{:S(2)}, u32[]{:S(2)}) %collective-permute-start) | collective-permute-done | bytes 30752 | tf_op jit(solution)/shard_map/ppermute | solution.py:81
  48.2 12.8 %collective-permute-start.2 = (bf16[24,640]{1,0:T(8,128)(2,1)S(1)}, bf16[24,640]{1,0:T(8,128)(2,1)S(1)}, u32[]{:S(2)}, u32[]{:S(2)}) collective-permute-start(bf16[24,640]{1,0:T(8,128)(2,1)S(1)} %bitcast.460), channel_id=1, source_target_pairs={{0,8},{1,9},{2,10},{3,11},{4,12},{5,13},{6,14},{7,15},{8,16},{9,17... | collective-permute-start | bytes 92168 | tf_op jit(solution)/shard_map/ppermute | solution.py:81
  75.3 7.7 %pick_rows.1 = bf16[16,64,768]{2,1,0:T(8,128)(2,1)} custom-call(s32[32]{0:T(128)} %pad_add_fusion.1.table, bf16[8,64,768]{2,1,0:T(8,128)(2,1)} %bitcast.442), custom_call_target="tpu_custom_call" | custom-call | tf_op jit(solution)/shard_map/pick_rows/pallas_call | solution.py:501
  106.4 15.0 %collective-permute-done.10 = bf16[256,640]{1,0:T(8,128)(2,1)S(1)} collective-permute-done((bf16[256,640]{1,0:T(8,128)(2,1)S(1)}, bf16[256,640]{1,0:T(8,128)(2,1)S(1)}, u32[]{:S(2)}, u32[]{:S(2)}) %collective-permute-start.10) | collective-permute-done | bytes 327712 | tf_op jit(solution)/shard_map/ppermute | solution.py:81
  129.3 18.6 %collective-permute-done.18 = bf16[4,64,768]{2,1,0:T(8,128)(2,1)S(1)} collective-permute-done((bf16[4,64,768]{2,1,0:T(8,128)(2,1)S(1)}, bf16[4,64,768]{2,1,0:T(8,128)(2,1)S(1)}, u32[]{:S(2)}, u32[]{:S(2)}) %collective-permute-start.18) | collective-permute-done | bytes 393248 | tf_op jit(solution)/shard_map/ppermute | solution.py:81
  171.6 10.2 %collective-permute-done.23 = bf16[64,768]{1,0:T(8,128)(2,1)S(1)} collective-permute-done((bf16[64,768]{1,0:T(8,128)(2,1)S(1)}, bf16[64,768]{1,0:T(8,128)(2,1)S(1)}, u32[]{:S(2)}, u32[]{:S(2)}) %collective-permute-start.23) | collective-permute-done | bytes 98336 | tf_op jit(solution)/shard_map/ppermute | solution.py:81
  183.6 10.6 %collective-permute-done.25 = bf16[4,64,768]{2,1,0:T(8,128)(2,1)S(1)} collective-permute-done((bf16[4,64,768]{2,1,0:T(8,128)(2,1)S(1)}, bf16[4,64,768]{2,1,0:T(8,128)(2,1)S(1)}, u32[]{:S(2)}, u32[]{:S(2)}) %collective-permute-start.25) | collective-permute-done | bytes 393248 | tf_op jit(solution)/shard_map/ppermute | solution.py:81
  196.6 42.7 %self_forward.1 = (f32[4,256,256]{2,1,0:T(8,128)}, f32[4,8,256]{2,1,0:T(8,128)}) custom-call(s32[25]{0:T(128)} %pad_add_fusion.table, bf16[2048,640]{1,0:T(8,128)(2,1)} %constant_dynamic-update-slice_fusion.7.own, bf16[2048,640]{1,0:T(8,128)(2,1)} %collective-permute-done.13.other), custom_call_target="tpu_custom_call" | custom-call | flops 3221225472 | bytes 5242880 | tf_op jit(solution)/shard_map/self_forward/pallas_call | solution.py:319
  248.4 9.4 %collective-permute-done.15 = bf16[256,256]{1,0:T(8,128)(2,1)S(1)} collective-permute-done((bf16[256,256]{1,0:T(8,128)(2,1)S(1)}, bf16[256,256]{1,0:T(8,128)(2,1)S(1)}, u32[]{:S(2)}, u32[]{:S(2)}) %collective-permute-start.15) | collective-permute-done | bytes 131104 | tf_op jit(solution)/shard_map/ppermute | solution.py:81
  269.5 11.1 %cross_forward.1 = (bf16[256,768]{1,0:T(8,128)(2,1)}, f32[6,8,256]{2,1,0:T(8,128)}) custom-call(bf16[256,768]{1,0:T(8,128)(2,1)} %fusion.37.query, bf16[1024,1536]{1,0:T(8,128)(2,1)} %add_convert_fusion.keys.values, bf16[1024,1536]{1,0:T(8,128)(2,1)} %add_convert_fusion.keys.values), custom_call_target="tpu_custom_call" | custom-call | flops 1610612736 | bytes 3145728 | tf_op jit(solution)/shard_map/cross_forward/pallas_call | solution.py:435
  287.8 9.7 %reshape.413 = bf16[32,24,4,768]{3,2,1,0:T(4,128)(2,1)} reshape(bf16[768,3072]{1,0:T(8,128)(2,1)} %slice.364) | data formatting | bytes 9437184 | tf_op jit(solution)/shard_map/reshape | solution.py:698
  300.8 10.1 %multiply_convert_fusion = (bf16[256,3072]{1,0:T(8,128)(2,1)S(1)}, f32[256,3072]{1,0:T(8,128)S(1)}, f32[256,3072]{1,0:T(8,128)S(1)}) fusion(f32[3072]{0:T(1024)S(1)} %add.782, bf16[768,6144]{1,0:T(8,128)(2,1)} %all-gather.5.cloned.1.call-done, f32[256,768]{1,0:T(8,128)S(1)} %get-tuple-element.220, f32[768]{0:T(1024)S(1)} %get-tuple-element.102, ...), kind=kOutput, calls=%fused_computation.25 | convolution fusion | flops 1260847104 | bytes 13389824 | tf_op jit(solution)/shard_map/dot_general | solution.py:45
  322.9 13.5 %cross_backward.1 = (bf16[256,768]{1,0:T(8,128)(2,1)}, bf16[1024,768]{1,0:T(8,128)(2,1)}, bf16[1024,768]{1,0:T(8,128)(2,1)}) custom-call(bf16[256,768]{1,0:T(8,128)(2,1)} %fusion.37.query, bf16[1024,1536]{1,0:T(8,128)(2,1)} %add_convert_fusion.keys.values, bf16[1024,1536]{1,0:T(8,128)(2,1)} %add_convert_fusion.keys.values, ...), custom_call_target="tpu_custom_call" | custom-call | flops 4026531840 | bytes 6291456 | tf_op jit(solution)/shard_map/cross_backward/pallas_call | solution.py:463
  393.3 44.5 %self_backward.1 = (bf16[2048,640]{1,0:T(8,128)(2,1)}, bf16[2048,640]{1,0:T(8,128)(2,1)}) custom-call(s32[25]{0:T(128)} %pad_add_fusion.table, bf16[2048,640]{1,0:T(8,128)(2,1)} %constant_dynamic-update-slice_fusion.7.own, bf16[2048,640]{1,0:T(8,128)(2,1)} %collective-permute-done.13.other, bf16[4,256,256]{2,1,0:T(8,128)(2,1)} %pad_maximum_fusion.4.dout, ...), custom_call_target="tpu_custom_call" | custom-call | flops 8053063680 | bytes 10485760 | tf_op jit(solution)/shard_map/self_backward/pallas_call | solution.py:350
  450.4 10.2 %collective-permute-done.36 = bf16[4,64,1536]{2,1,0:T(8,128)(2,1)S(1)} collective-permute-done((bf16[4,64,1536]{2,1,0:T(8,128)(2,1)S(1)}, bf16[4,64,1536]{2,1,0:T(8,128)(2,1)S(1)}, u32[]{:S(2)}, u32[]{:S(2)}) %collective-permute-start.36) | collective-permute-done | bytes 786464 | tf_op jit(solution)/shard_map/ppermute | solution.py:81
  498.4 7.5 %collective-permute-start.62 = (bf16[4,2,24,1536]{3,2,0,1:T(8,128)(2,1)S(1)}, bf16[4,2,24,1536]{3,2,0,1:T(8,128)(2,1)S(1)}, u32[]{:S(2)}, u32[]{:S(2)}) collective-permute-start(bf16[4,2,24,1536]{3,2,0,1:T(8,128)(2,1)S(1)} %copy-done.36), channel_id=1, source_target_pairs={{0,1},{1,0},{2,3},{3,2},{4,5},{5,4},{6,7},{7,6},{8,9},{9,8},{10,11... | collective-permute-start | bytes 1769480 | tf_op jit(solution)/shard_map/ppermute | solution.py:81
  513.4 8.8 %collective-permute-done.68 = bf16[4,2,96,384]{3,2,0,1:T(8,128)(2,1)S(1)} collective-permute-done((bf16[4,2,96,384]{3,2,0,1:T(8,128)(2,1)S(1)}, bf16[4,2,96,384]{3,2,0,1:T(8,128)(2,1)S(1)}, u32[]{:S(2)}, u32[]{:S(2)}) %collective-permute-start.68) | collective-permute-done | bytes 589856 | tf_op jit(solution)/shard_map/ppermute | solution.py:81
  523.0 9.8 %collective-permute-done.70 = bf16[4,2,96,384]{3,2,0,1:T(8,128)(2,1)S(1)} collective-permute-done((bf16[4,2,96,384]{3,2,0,1:T(8,128)(2,1)S(1)}, bf16[4,2,96,384]{3,2,0,1:T(8,128)(2,1)S(1)}, u32[]{:S(2)}, u32[]{:S(2)}) %collective-permute-start.70) | collective-permute-done | bytes 589856 | tf_op jit(solution)/shard_map/ppermute | solution.py:81
  536.7 7.5 %collective-permute-done.69 = bf16[4,96,384]{2,1,0:T(8,128)(2,1)S(1)} collective-permute-done((bf16[4,96,384]{2,1,0:T(8,128)(2,1)S(1)}, bf16[4,96,384]{2,1,0:T(8,128)(2,1)S(1)}, u32[]{:S(2)}, u32[]{:S(2)}) %collective-permute-start.69) | collective-permute-done | bytes 294944 | tf_op jit(solution)/shard_map/ppermute | solution.py:81
  544.3 20.7 %collective-permute-done.71 = bf16[4,96,384]{2,1,0:T(8,128)(2,1)S(1)} collective-permute-done((bf16[4,96,384]{2,1,0:T(8,128)(2,1)S(1)}, bf16[4,96,384]{2,1,0:T(8,128)(2,1)S(1)}, u32[]{:S(2)}, u32[]{:S(2)}) %collective-permute-start.71) | collective-permute-done | bytes 294944 | tf_op jit(solution)/shard_map/ppermute | solution.py:81
  573.3 8.8 %collective-permute-done.73 = bf16[96,768]{1,0:T(8,128)(2,1)S(1)} collective-permute-done((bf16[96,768]{1,0:T(8,128)(2,1)S(1)}, bf16[96,768]{1,0:T(8,128)(2,1)S(1)}, u32[]{:S(2)}, u32[]{:S(2)}) %collective-permute-start.73) | collective-permute-done | bytes 147488 | tf_op jit(solution)/shard_map/ppermute | solution.py:81
  582.9 6.8 collective-permute-done.65
  627.2 12.7 %collective-permute-done.33 = bf16[256,768]{1,0:T(8,128)(2,1)} collective-permute-done((bf16[256,768]{1,0:T(8,128)(2,1)}, bf16[256,768]{1,0:T(8,128)(2,1)}, u32[]{:S(2)}, u32[]{:S(2)}) %collective-permute-start.33) | collective-permute-done | bytes 393248 | tf_op jit(solution)/shard_map/ppermute | solution.py:81
  655.6 14.9 %collective-permute-done.52 = bf16[4,2,24,1920]{3,2,1,0:T(8,128)(2,1)} collective-permute-done((bf16[4,2,24,1920]{3,2,1,0:T(8,128)(2,1)}, bf16[4,2,24,1920]{3,2,1,0:T(8,128)(2,1)}, u32[]{:S(2)}, u32[]{:S(2)}) %collective-permute-start.52) | collective-permute-done | bytes 737312 | tf_op jit(solution)/shard_map/ppermute | solution.py:81
  (510 shorter events, 345.8 us)
Async XLA Ops:
  7.2 251.0 %all-gather.3.cloned.1.call-start = ((), (), s32[]{:S(2)}) async-start(), calls=%async_computation | async-start | bytes 6285312 | tf_op jit(solution)/shard_map/all_gather | solution.py:584
  12.0 271.0 %all-gather.5.cloned.1.call-start = ((), (), s32[]{:S(2)}) async-start(), calls=%async_computation.1 | async-start | bytes 9732096 | tf_op jit(solution)/shard_map/all_gather | solution.py:585
  14.6 80.7 %collective-permute-start.6 = (bf16[256,768]{1,0:T(8,128)(2,1)}, bf16[256,768]{1,0:T(8,128)(2,1)}, u32[]{:S(2)}, u32[]{:S(2)}) collective-permute-start(bf16[256,768]{1,0:T(8,128)(2,1)} %bitcast.450), channel_id=1, source_target_pairs={{0,8},{1,9},{2,10},{3,11},{4,12},{5,13},{6,14},{7,15},{8,16},{9,17... | collective-permute-start | bytes 1179656 | tf_op jit(solution)/shard_map/ppermute | solution.py:81
  17.7 84.2 %collective-permute-start.8 = (bf16[256,768]{1,0:T(8,128)(2,1)}, bf16[256,768]{1,0:T(8,128)(2,1)}, u32[]{:S(2)}, u32[]{:S(2)}) collective-permute-start(bf16[256,768]{1,0:T(8,128)(2,1)} %bitcast.451), channel_id=1, source_target_pairs={{0,24},{1,25},{2,26},{3,27},{4,28},{5,29},{6,30},{7,31},{8,0},{9,1... | collective-permute-start | bytes 1179656 | tf_op jit(solution)/shard_map/ppermute | solution.py:81
  19.8 77.8 %collective-permute-start.7 = (bf16[256,768]{1,0:T(8,128)(2,1)}, bf16[256,768]{1,0:T(8,128)(2,1)}, u32[]{:S(2)}, u32[]{:S(2)}) collective-permute-start(bf16[256,768]{1,0:T(8,128)(2,1)} %bitcast.452), channel_id=1, source_target_pairs={{0,16},{1,17},{2,18},{3,19},{4,20},{5,21},{6,22},{7,23},{8,24},{9,... | collective-permute-start | bytes 1179656 | tf_op jit(solution)/shard_map/ppermute | solution.py:81
  24.8 36.9 %collective-permute-start.1 = (bf16[24,640]{1,0:T(8,128)(2,1)S(1)}, bf16[24,640]{1,0:T(8,128)(2,1)S(1)}, u32[]{:S(2)}, u32[]{:S(2)}) collective-permute-start(bf16[24,640]{1,0:T(8,128)(2,1)S(1)} %bitcast.458), channel_id=1, source_target_pairs={{0,16},{1,17},{2,18},{3,19},{4,20},{5,21},{6,22},{7,23},{8,24},{9,... | collective-permute-start | bytes 92168 | tf_op jit(solution)/shard_map/ppermute | solution.py:81
  84.2 44.2 %collective-permute-start.17 = (bf16[4,2,64,768]{3,2,1,0:T(8,128)(2,1)S(1)}, bf16[4,2,64,768]{3,2,1,0:T(8,128)(2,1)S(1)}, u32[]{:S(2)}, u32[]{:S(2)}) collective-permute-start(bf16[4,2,64,768]{3,2,1,0:T(8,128)(2,1)S(1)} %dynamic-slice_bitcast_fusion.2), channel_id=1, source_target_pairs={{0,2},{1,3},{2,0},{3,1},{4,6},{5,7},{6,4},{7,5},{8,10},{9,11},{10,... | collective-permute-start | bytes 2359304 | tf_op jit(solution)/shard_map/ppermute | solution.py:81
  128.4 68.2 %collective-permute-start.13 = (bf16[2048,640]{1,0:T(8,128)(2,1)}, bf16[2048,640]{1,0:T(8,128)(2,1)}, u32[]{:S(2)}, u32[]{:S(2)}) collective-permute-start(bf16[2048,640]{1,0:T(8,128)(2,1)} %constant_dynamic-update-slice_fusion.7.own), channel_id=1, source_target_pairs={{0,2},{1,3},{2,0},{3,1},{4,6},{5,7},{6,4},{7,5},{8,10},{9,11},{10,... | collective-permute-start | bytes 7864328 | tf_op jit(solution)/shard_map/ppermute | solution.py:81
  195.2 48.9 %collective-permute-start.26 = (bf16[2,4,64,768]{3,2,1,0:T(8,128)(2,1)}, bf16[2,4,64,768]{3,2,1,0:T(8,128)(2,1)}, u32[]{:S(2)}, u32[]{:S(2)}) collective-permute-start(bf16[2,4,64,768]{3,2,1,0:T(8,128)(2,1)} %get-tuple-element.157), channel_id=1, source_target_pairs={{0,2},{1,3},{2,0},{3,1},{4,6},{5,7},{6,4},{7,5},{8,10},{9,11},{10,... | collective-permute-start | bytes 2359304 | tf_op jit(solution)/shard_map/ppermute | solution.py:81
  359.7 31.7 %collective-permute-start.27 = (bf16[256,256]{1,0:T(8,128)(2,1)}, bf16[256,256]{1,0:T(8,128)(2,1)}, u32[]{:S(2)}, u32[]{:S(2)}) collective-permute-start(bf16[256,256]{1,0:T(8,128)(2,1)} %get-tuple-element.168), channel_id=1, source_target_pairs={{0,14},{1,15},{2,12},{3,13},{4,10},{5,11},{6,8},{7,9},{8,22},{9,23... | collective-permute-start | bytes 393224 | tf_op jit(solution)/shard_map/ppermute | solution.py:81
  359.7 31.7 %collective-permute-start.28 = (bf16[256,256]{1,0:T(8,128)(2,1)}, bf16[256,256]{1,0:T(8,128)(2,1)}, u32[]{:S(2)}, u32[]{:S(2)}) collective-permute-start(bf16[256,256]{1,0:T(8,128)(2,1)} %get-tuple-element.169), channel_id=1, source_target_pairs={{0,16},{1,17},{2,18},{3,19},{4,20},{5,21},{6,22},{7,23},{8,24},{9,... | collective-permute-start | bytes 393224 | tf_op jit(solution)/shard_map/ppermute | solution.py:81
  360.8 30.7 %collective-permute-start.29 = (bf16[256,256]{1,0:T(8,128)(2,1)}, bf16[256,256]{1,0:T(8,128)(2,1)}, u32[]{:S(2)}, u32[]{:S(2)}) collective-permute-start(bf16[256,256]{1,0:T(8,128)(2,1)} %get-tuple-element.170), channel_id=1, source_target_pairs={{0,30},{1,31},{2,28},{3,29},{4,26},{5,27},{6,24},{7,25},{8,6},{9,7... | collective-permute-start | bytes 393224 | tf_op jit(solution)/shard_map/ppermute | solution.py:81
  367.7 70.1 %collective-permute-start.35 = (bf16[2,4,64,1536]{3,2,1,0:T(8,128)(2,1)}, bf16[2,4,64,1536]{3,2,1,0:T(8,128)(2,1)}, u32[]{:S(2)}, u32[]{:S(2)}) collective-permute-start(bf16[2,4,64,1536]{3,2,1,0:T(8,128)(2,1)} %bitcast.78), channel_id=1, source_target_pairs={{0,2},{1,3},{2,0},{3,1},{4,6},{5,7},{6,4},{7,5},{8,10},{9,11},{10,... | collective-permute-start | bytes 4718600 | tf_op jit(solution)/shard_map/ppermute | solution.py:81
  381.6 58.6 %collective-permute-start.59 = (bf16[4,2,2,24,3072]{4,3,0,1,2:T(8,128)(2,1)}, bf16[4,2,2,24,3072]{4,3,0,1,2:T(8,128)(2,1)}, u32[]{:S(2)}, u32[]{:S(2)}) collective-permute-start(bf16[4,2,2,24,3072]{4,3,0,1,2:T(8,128)(2,1)} %bitcast.400), channel_id=1, source_target_pairs={{0,2},{1,3},{2,0},{3,1},{4,6},{5,7},{6,4},{7,5},{8,10},{9,11},{10,... | collective-permute-start | bytes 7077896 | tf_op jit(solution)/shard_map/ppermute | solution.py:81
  391.4 54.5 %collective-permute-start.67 = (bf16[4,2,2,96,768]{4,3,0,1,2:T(8,128)(2,1)}, bf16[4,2,2,96,768]{4,3,0,1,2:T(8,128)(2,1)}, u32[]{:S(2)}, u32[]{:S(2)}) collective-permute-start(bf16[4,2,2,96,768]{4,3,0,1,2:T(8,128)(2,1)} %bitcast.399), channel_id=1, source_target_pairs={{0,2},{1,3},{2,0},{3,1},{4,6},{5,7},{6,4},{7,5},{8,10},{9,11},{10,... | collective-permute-start | bytes 7077896 | tf_op jit(solution)/shard_map/ppermute | solution.py:81
  437.8 69.6 %collective-permute-start.30 = (bf16[2048,640]{1,0:T(8,128)(2,1)}, bf16[2048,640]{1,0:T(8,128)(2,1)}, u32[]{:S(2)}, u32[]{:S(2)}) collective-permute-start(bf16[2048,640]{1,0:T(8,128)(2,1)} %get-tuple-element.28), channel_id=1, source_target_pairs={{0,2},{1,3},{2,0},{3,1},{4,6},{5,7},{6,4},{7,5},{8,10},{9,11},{10,... | collective-permute-start | bytes 7864328 | tf_op jit(solution)/shard_map/ppermute | solution.py:81
  443.9 66.3 %collective-permute-start.60 = (bf16[4,2,24,1536]{3,2,0,1:T(8,128)(2,1)}, bf16[4,2,24,1536]{3,2,0,1:T(8,128)(2,1)}, u32[]{:S(2)}, u32[]{:S(2)}) collective-permute-start(bf16[4,2,24,1536]{3,2,0,1:T(8,128)(2,1)} %dynamic-slice_bitcast_fusion.7), channel_id=1, source_target_pairs={{0,4},{1,5},{2,6},{3,7},{4,0},{5,1},{6,2},{7,3},{8,12},{9,13},{10,... | collective-permute-start | bytes 1769480 | tf_op jit(solution)/shard_map/ppermute | solution.py:81
  506.2 26.6 %collective-permute-start.70 = (bf16[4,2,96,384]{3,2,0,1:T(8,128)(2,1)S(1)}, bf16[4,2,96,384]{3,2,0,1:T(8,128)(2,1)S(1)}, u32[]{:S(2)}, u32[]{:S(2)}) collective-permute-start(bf16[4,2,96,384]{3,2,0,1:T(8,128)(2,1)S(1)} %copy-done.34), channel_id=1, source_target_pairs={{0,1},{1,0},{2,3},{3,2},{4,5},{5,4},{6,7},{7,6},{8,9},{9,8},{10,11... | collective-permute-start | bytes 1769480 | tf_op jit(solution)/shard_map/ppermute | solution.py:81
  507.4 141.1 %collective-permute-start.51 = (bf16[4,2,2,24,3968]{4,3,2,1,0:T(8,128)(2,1)}, bf16[4,2,2,24,3968]{4,3,2,1,0:T(8,128)(2,1)}, u32[]{:S(2)}, u32[]{:S(2)}) collective-permute-start(bf16[4,2,2,24,3968]{4,3,2,1,0:T(8,128)(2,1)} %dynamic-slice_bitcast_fusion), channel_id=1, source_target_pairs={{0,2},{1,3},{2,0},{3,1},{4,6},{5,7},{6,4},{7,5},{8,10},{9,11},{10,... | collective-permute-start | bytes 9142280 | tf_op jit(solution)/shard_map/ppermute | solution.py:81
  522.2 69.4 %collective-permute-start.31 = (bf16[4,256,640]{2,1,0:T(8,128)(2,1)S(1)}, bf16[4,256,640]{2,1,0:T(8,128)(2,1)S(1)}, u32[]{:S(2)}, u32[]{:S(2)}) collective-permute-start(bf16[4,256,640]{2,1,0:T(8,128)(2,1)S(1)} %bitcast.438), channel_id=1, source_target_pairs={{0,4},{1,5},{2,6},{3,7},{4,0},{5,1},{6,2},{7,3},{8,12},{9,13},{10,... | collective-permute-start | bytes 3932168 | tf_op jit(solution)/shard_map/ppermute | solution.py:81
  522.7 45.5 %collective-permute-start.61 = (bf16[4,24,1536]{2,1,0:T(8,128)(2,1)S(1)}, bf16[4,24,1536]{2,1,0:T(8,128)(2,1)S(1)}, u32[]{:S(2)}, u32[]{:S(2)}) collective-permute-start(bf16[4,24,1536]{2,1,0:T(8,128)(2,1)S(1)} %dynamic-slice_bitcast_fusion.15), channel_id=1, source_target_pairs={{0,1},{1,0},{2,3},{3,2},{4,5},{5,4},{6,7},{7,6},{8,9},{9,8},{10,11... | collective-permute-start | bytes 884744 | tf_op jit(solution)/shard_map/ppermute | solution.py:81
  535.1 30.0 %collective-permute-start.71 = (bf16[4,96,384]{2,1,0:T(8,128)(2,1)S(1)}, bf16[4,96,384]{2,1,0:T(8,128)(2,1)S(1)}, u32[]{:S(2)}, u32[]{:S(2)}) collective-permute-start(bf16[4,96,384]{2,1,0:T(8,128)(2,1)S(1)} %dynamic-slice_bitcast_fusion.12), channel_id=1, source_target_pairs={{0,4},{1,5},{2,6},{3,7},{4,0},{5,1},{6,2},{7,3},{8,12},{9,13},{10,... | collective-permute-start | bytes 884744 | tf_op jit(solution)/shard_map/ppermute | solution.py:81
  582.9 31.0 %collective-permute-start.44 = (bf16[2,4,64,768]{3,2,1,0:T(8,128)(2,1)}, bf16[2,4,64,768]{3,2,1,0:T(8,128)(2,1)}, u32[]{:S(2)}, u32[]{:S(2)}) collective-permute-start(bf16[2,4,64,768]{3,2,1,0:T(8,128)(2,1)} %get-tuple-element.152), channel_id=1, source_target_pairs={{0,2},{1,3},{2,0},{3,1},{4,6},{5,7},{6,4},{7,5},{8,10},{9,11},{10,... | collective-permute-start | bytes 2359304 | tf_op jit(solution)/shard_map/ppermute | solution.py:81
  604.8 35.0 %collective-permute-start.33 = (bf16[256,768]{1,0:T(8,128)(2,1)}, bf16[256,768]{1,0:T(8,128)(2,1)}, u32[]{:S(2)}, u32[]{:S(2)}) collective-permute-start(bf16[256,768]{1,0:T(8,128)(2,1)} %convolution_convert_fusion.7), channel_id=1, source_target_pairs={{0,16},{1,17},{2,18},{3,19},{4,20},{5,21},{6,22},{7,23},{8,24},{9,... | collective-permute-start | bytes 1179656 | tf_op jit(solution)/shard_map/ppermute | solution.py:81
  (103 other events, 1184.0 us)
Sparse Core Ops, SparseCore 0:
  12.1 88.3 all-gather.2
  104.0 98.7 all-gather.4
